TPU v7x, 32 devices: a whole 2x2x4 slice. The times are simulated.
32 devices in a mesh: dp: 16 (over z, y, core), tensor: 2 (over x).
Axes of the slice: x: 2, y: 2, z: 4, core: 2. Of those that a mesh axis runs over, the one named last changes fastest.
Arguments:
- tokens: bfloat16 [32, 1024, 1024], P('dp'), may hold values from -6 to 6
- d_output: bfloat16 [32, 1024, 1024], P('dp'), may hold values from -6 to 6
- lengths: int32 [32], P('dp'), may hold values from 256 to 1024, as said below
- ln1_gain: bfloat16 [1024], replicated, may hold values from 0.5 to 1.5
- ln1_bias: bfloat16 [1024], replicated, may hold values from -4 to 4
- w_qkv: bfloat16 [1024, 3, 1024], P(None, None, 'tensor'), may hold values from -0.1875 to 0.1875
- qv_bias: bfloat16 [2, 1024], P(None, 'tensor'), may hold values from -4 to 4
- w_out: bfloat16 [1024, 1024], P('tensor'), may hold values from -0.75 to 0.75
- bias_out: bfloat16 [1024], replicated, may hold values from -4 to 4
- ln2_gain: bfloat16 [1024], replicated, may hold values from 0.5 to 1.5
- ln2_bias: bfloat16 [1024], replicated, may hold values from -4 to 4
- w_up: bfloat16 [1024, 4096], P(None, 'tensor'), may hold values from -0.1875 to 0.1875
- b_up: bfloat16 [4096], P('tensor'), may hold values from -6 to 6
- w_down: bfloat16 [4096, 1024], P('tensor'), may hold values from -0.09375 to 0.09375
- b_down: bfloat16 [1024], replicated, may hold values from -4 to 4
Outputs:
- output: bfloat16 [32, 1024, 1024], P('dp', 'tensor')
- grad_tokens: bfloat16 [32, 1024, 1024], P('dp', 'tensor')
- grad_ln1_gain: float32 [1024], replicated
- grad_ln1_bias: float32 [1024], replicated
- grad_w_qkv: float32 [1024, 3, 1024], P(None, None, 'tensor')
- grad_qv_bias: float32 [2, 1024], P(None, 'tensor')
- grad_w_out: float32 [1024, 1024], P('tensor')
- grad_bias_out: float32 [1024], replicated
- grad_ln2_gain: float32 [1024], replicated
- grad_ln2_bias: float32 [1024], replicated
- grad_w_up: float32 [1024, 4096], P(None, 'tensor')
- grad_b_up: float32 [4096], P('tensor')
- grad_w_down: float32 [4096, 1024], P('tensor')
- grad_b_down: float32 [1024], replicated
Inputs may be any that keep to these rules, and one draw needn't show every extreme that they name: A sequence's valid slots are its first lengths[b]; at least one sequence has all 1024 slots valid.
All inputs are finite; a program needn't handle non-finite values.
Results may differ from a plain program's by a relative error of at most 0.02.
Values may be sent and summed in bfloat16 or wider, within the bound.
A program may use at most 384 MiB of HBM per device.

v0:
```python
import functools
import math

import jax
import jax.numpy as jnp
import numpy as np
from jax import lax
from jax.experimental import pallas as pl
from jax.experimental.pallas import tpu as pltpu
from jax.sharding import PartitionSpec as P

HEADS = 16
HEAD_DIM = 64


epsilon = 1e-05
root_two_pi = math.sqrt(2.0 / math.pi)
masked_score = -1e30


def matmul(left, right):
    return jnp.dot(left, right, preferred_element_type=jnp.float32)


def contract_rows(left, right):
    return lax.dot_general(
        left, right, (((0,), (0,)), ((), ())), preferred_element_type=jnp.float32
    )


def contract_cols(left, right):
    return lax.dot_general(
        left, right, (((1,), (1,)), ((), ())), preferred_element_type=jnp.float32
    )


def norm_parts(values):
    centre = jnp.mean(values, -1, keepdims=True)
    shifted = values - centre
    inverse = lax.rsqrt(jnp.mean(shifted * shifted, -1, keepdims=True) + epsilon)
    return (shifted * inverse, inverse)


def norm_backward(grad_normed, normal, inverse, gain):
    scaled = grad_normed * gain
    return inverse * (
        scaled
        - jnp.mean(scaled, -1, keepdims=True)
        - normal * jnp.mean(scaled * normal, -1, keepdims=True)
    )


def gelu_parts(pre):
    tangent = jnp.tanh(root_two_pi * (pre + 0.044715 * pre * pre * pre))
    value = 0.5 * pre * (1.0 + tangent)
    slope = 0.5 * (1.0 + tangent) + 0.5 * pre * (1.0 - tangent * tangent) * root_two_pi * (
        1.0 + 3.0 * 0.044715 * pre * pre
    )
    return (value, slope)


def block_probs(query_rows, key_rows, start, length, slopes, scale):
    rows = query_rows.shape[0]
    cols = key_rows.shape[0]
    products = jnp.einsum("ihd,jhd->hij", query_rows, key_rows, preferred_element_type=jnp.float32)
    key_place = jnp.arange(cols, dtype=jnp.int32)
    distance = (start + jnp.arange(rows, dtype=jnp.int32))[:, None] - key_place[None, :]
    scores = products * scale - slopes[:, None, None] * distance.astype(jnp.float32)[None]
    allowed = (distance >= 0) & (key_place[None, :] < length)
    masked = jnp.where(allowed[None], scores, masked_score)
    highest = jnp.max(masked, -1, keepdims=True)
    exponent = jnp.exp(masked - highest)
    return exponent / jnp.sum(exponent, -1, keepdims=True)


def attention_forward(query, keys, values, length, slopes, scale):
    slots = query.shape[0]
    block = min(512, slots)
    outputs = []
    for number in range(slots // block):
        start = number * block
        probs = block_probs(query[start : start + block], keys, start, length, slopes, scale)
        mixed = jnp.einsum(
            "hij,jhd->ihd", probs.astype(jnp.bfloat16), values, preferred_element_type=jnp.float32
        )
        outputs.append(mixed.reshape(block, -1).astype(jnp.bfloat16))
    return jnp.concatenate(outputs, 0)


def attention_backward(query, keys, values, grad_attn, length, slopes, scale):
    slots, heads_local, head_width = query.shape
    block = min(512, slots)
    grad_keys = jnp.zeros((slots, heads_local, head_width), jnp.float32)
    grad_values = jnp.zeros((slots, heads_local, head_width), jnp.float32)
    query_parts = []
    for number in range(slots // block):
        start = number * block
        query_rows = query[start : start + block]
        grad_rows = grad_attn[start : start + block]
        probs = block_probs(query_rows, keys, start, length, slopes, scale)
        grad_probs = jnp.einsum(
            "ihd,jhd->hij", grad_rows, values, preferred_element_type=jnp.float32
        )
        delta = jnp.sum(probs * grad_probs, -1, keepdims=True)
        grad_scores = (probs * (grad_probs - delta)).astype(jnp.bfloat16)
        part_query = (
            jnp.einsum("hij,jhd->ihd", grad_scores, keys, preferred_element_type=jnp.float32)
            * scale
        )
        part_keys = (
            jnp.einsum("hij,ihd->jhd", grad_scores, query_rows, preferred_element_type=jnp.float32)
            * scale
        )
        part_values = jnp.einsum(
            "hij,ihd->jhd",
            probs.astype(jnp.bfloat16),
            grad_rows,
            preferred_element_type=jnp.float32,
        )
        part_query, part_keys, part_values = (part_query, part_keys, part_values)
        query_parts.append(part_query)
        grad_keys = grad_keys.at[:slots].add(part_keys)
        grad_values = grad_values.at[:slots].add(part_values)
    grad_query = jnp.concatenate(query_parts, 0).reshape(slots, -1).astype(jnp.bfloat16)
    return (
        grad_query,
        grad_keys.reshape(slots, -1).astype(jnp.bfloat16),
        grad_values.reshape(slots, -1).astype(jnp.bfloat16),
    )


QUERY_BLOCK = 256
KEY_BLOCK = 1024
PAIR = 128
NT = (((1,), (1,)), ((), ()))
TN = (((0,), (0,)), ((), ()))


def mm(left, right, dims=(((1,), (0,)), ((), ()))):
    return lax.dot_general(left, right, dims, preferred_element_type=jnp.float32)


def low_lanes(rows):
    return lax.broadcasted_iota(jnp.int32, (rows, PAIR), 1) < HEAD_DIM


def slope_rows():
    table = np.zeros((HEADS // 2, 8, PAIR), np.float64)
    for head in range(HEADS):
        rest = np.float64(np.float32(2.0 ** (-8.0 * (head + 1) / HEADS)))
        base = HEAD_DIM * (1 - head % 2)
        for part in range(3):
            piece = np.float64(np.asarray(rest).astype(jnp.bfloat16))
            rest = rest - piece
            table[head // 2, head % 2, base + part] = 32.0 * piece
            table[head // 2, head % 2, base + 3 + part] = piece
        table[head // 2, head % 2, base + 6] = 1.0
    return table.astype(jnp.bfloat16)


def key_lanes(slots, length):
    place = jnp.arange(slots, dtype=jnp.int32)[:, None]
    lane = jnp.arange(PAIR, dtype=jnp.int32)[None, :] % HEAD_DIM
    high = (place // 32).astype(jnp.float32)
    low = (place % 32).astype(jnp.float32)
    mask = jnp.where(place < length, 0.0, masked_score)
    return jnp.where(
        lane < 3, high, jnp.where(lane < 6, low, jnp.where(lane == 6, mask, 0.0))
    ).astype(jnp.bfloat16)


def forward_kernel(
    q_ref, k_ref, v_ref, lanes_ref, rows_ref, o_ref, level_ref, key0, key1, val0, val1
):
    slots = q_ref.shape[0]
    block = QUERY_BLOCK
    low = low_lanes(slots)
    zero = jnp.zeros((slots, PAIR), jnp.bfloat16)
    one = jnp.ones((slots, PAIR), jnp.bfloat16)
    key0[...] = jnp.where(low, k_ref[...], lanes_ref[...])
    key1[...] = jnp.where(low, lanes_ref[...], k_ref[...])
    val0[:, :PAIR] = jnp.where(low, v_ref[...], zero)
    val0[:, PAIR:] = jnp.where(low, one, zero)
    val1[:, :PAIR] = jnp.where(low, zero, v_ref[...])
    val1[:, PAIR:] = jnp.where(low, zero, one)
    low_block = low_lanes(block)
    causal = lax.broadcasted_iota(jnp.int32, (block, block), 1) <= lax.broadcasted_iota(
        jnp.int32, (block, block), 0
    )
    for number in range(slots // block):
        start = number * block
        rows = q_ref[start : start + block, :] * jnp.bfloat16(0.125)
        total = None
        tops = []
        for head, (key, val) in enumerate(((key0, val0), (key1, val1))):
            extra = jnp.broadcast_to(rows_ref[0, head : head + 1, :], (block, PAIR))
            query = jnp.where(low_block, rows, extra) if head == 0 else jnp.where(
                low_block, extra, rows
            )
            own = jnp.where(causal, mm(query, key[start : start + block, :], NT), masked_score)
            highest = jnp.max(own, 1, keepdims=True)
            if start:
                past = mm(query, key[:start, :], NT)
                highest = jnp.maximum(highest, jnp.max(past, 1, keepdims=True))
                part = mm(jnp.exp(past - highest).astype(jnp.bfloat16), val[:start, :])
                total = part if total is None else total + part
            part = mm(jnp.exp(own - highest).astype(jnp.bfloat16), val[start : start + block, :])
            total = part if total is None else total + part
            tops.append(highest)
        o_ref[start : start + block, :] = (total[:, :PAIR] / total[:, PAIR:]).astype(jnp.bfloat16)
        level = (jnp.where(low_block, tops[0], tops[1]) + jnp.log(total[:, PAIR:])).T
        level_ref[0, 0:1, start : start + block] = level[0:1, :]
        level_ref[0, 1:2, start : start + block] = level[HEAD_DIM : HEAD_DIM + 1, :]


def backward_kernel(
    q_ref, k_ref, v_ref, o_ref, g_ref, level_ref, lanes_ref, rows_ref, dq_ref, dk_ref, dv_ref,
    key0, key1, val0, val1, bare0, bare1, total_k, total_v,
):
    slots = q_ref.shape[0]
    block = QUERY_BLOCK
    piece = KEY_BLOCK
    low = low_lanes(slots)
    zero = jnp.zeros((slots, PAIR), jnp.bfloat16)
    key0[...] = jnp.where(low, k_ref[...], lanes_ref[...])
    key1[...] = jnp.where(low, lanes_ref[...], k_ref[...])
    bare0[...] = jnp.where(low, k_ref[...], zero)
    bare1[...] = jnp.where(low, zero, k_ref[...])
    val0[...] = jnp.where(low, v_ref[...], zero)
    val1[...] = jnp.where(low, zero, v_ref[...])
    low_block = low_lanes(block)
    nil = jnp.zeros((block, PAIR), jnp.bfloat16)
    causal = lax.broadcasted_iota(jnp.int32, (block, block), 0) <= lax.broadcasted_iota(
        jnp.int32, (block, block), 1
    )
    for number in reversed(range(slots // block)):
        start = number * block
        stop = start + block
        rows = q_ref[start:stop, :] * jnp.bfloat16(0.125)
        grad = g_ref[start:stop, :]
        shares = (grad.astype(jnp.float32) * o_ref[start:stop, :].astype(jnp.float32)).T
        deltas = [
            jnp.sum(shares[head * HEAD_DIM : (head + 1) * HEAD_DIM, :], 0, keepdims=True)
            for head in range(2)
        ]
        levels = [level_ref[0, head : head + 1, start:stop] for head in range(2)]
        extras = [jnp.broadcast_to(rows_ref[0, h : h + 1, :], (block, PAIR)) for h in range(2)]
        queries = (
            jnp.where(low_block, rows, extras[0]),
            jnp.where(low_block, extras[1], rows),
        )
        grads = jnp.concatenate(
            [jnp.where(low_block, grad, nil), jnp.where(low_block, nil, grad)], 0
        )
        both = jnp.concatenate(
            [jnp.where(low_block, rows, nil), jnp.where(low_block, nil, rows)], 0
        )
        grad_query = None
        for begin in range(0, stop, min(piece, stop)):
            end = min(begin + piece, stop)
            probs, scores = [], []
            for head, (key, val, bare) in enumerate(((key0, val0, bare0), (key1, val1, bare1))):
                score = mm(key[begin:end, :], queries[head], NT)
                if end > start:
                    own = jnp.where(causal, score[start - begin :], masked_score)
                    score = jnp.concatenate([score[: start - begin], own], 0) if start > begin else own
                prob = jnp.exp(score - levels[head])
                grad_prob = mm(val[begin:end, :], grad, NT)
                grad_score = (prob * (grad_prob - deltas[head])).astype(jnp.bfloat16)
                probs.append(prob.astype(jnp.bfloat16))
                scores.append(grad_score)
                part = mm(grad_score, bare[begin:end, :], TN)
                grad_query = part if grad_query is None else grad_query + part
            part_v = mm(jnp.concatenate(probs, 1), grads)
            part_k = mm(jnp.concatenate(scores, 1), both)
            if stop == slots:
                total_v[begin:end, :] = part_v
                total_k[begin:end, :] = part_k
            else:
                total_v[begin:end, :] += part_v
                total_k[begin:end, :] += part_k
        dq_ref[start:stop, :] = (grad_query * 0.125).astype(jnp.bfloat16)
    dk_ref[...] = total_k[...].astype(jnp.bfloat16)
    dv_ref[...] = total_v[...].astype(jnp.bfloat16)


def pair_specs(slots):
    part = pl.BlockSpec((slots, PAIR), lambda pair: (0, pair))
    lanes = pl.BlockSpec((slots, PAIR), lambda pair: (0, 0))
    rows = pl.BlockSpec((1, 8, PAIR), lambda pair: (pair, 0, 0))
    levels = pl.BlockSpec((1, 8, slots), lambda pair: (pair, 0, 0))
    return part, lanes, rows, levels


def attention_out(query, keys, values, lanes, rows):
    slots, columns = query.shape
    part, lane_spec, row_spec, level_spec = pair_specs(slots)
    pairs = columns // PAIR
    half = slots * slots * PAIR * pairs
    return pl.pallas_call(
        forward_kernel,
        grid=(pairs,),
        out_shape=(
            jax.ShapeDtypeStruct((slots, columns), jnp.bfloat16),
            jax.ShapeDtypeStruct((pairs, 8, slots), jnp.float32),
        ),
        in_specs=[part, part, part, lane_spec, row_spec],
        out_specs=(part, level_spec),
        scratch_shapes=[pltpu.VMEM((slots, PAIR), jnp.bfloat16)] * 2
        + [pltpu.VMEM((slots, 2 * PAIR), jnp.bfloat16)] * 2,
        cost_estimate=pl.CostEstimate(
            flops=8 * half, bytes_accessed=8 * slots * columns, transcendentals=slots * slots * pairs
        ),
        name="attention_out",
    )(query, keys, values, lanes, rows)


def attention_grads(query, keys, values, mixed, levels, grad, lanes, rows):
    slots, columns = query.shape
    part, lane_spec, row_spec, level_spec = pair_specs(slots)
    pairs = columns // PAIR
    half = slots * slots * PAIR * pairs
    shape = jax.ShapeDtypeStruct((slots, columns), jnp.bfloat16)
    return pl.pallas_call(
        backward_kernel,
        grid=(pairs,),
        out_shape=(shape, shape, shape),
        in_specs=[part, part, part, part, part, level_spec, lane_spec, row_spec],
        out_specs=(part, part, part),
        scratch_shapes=[pltpu.VMEM((slots, PAIR), jnp.bfloat16)] * 6
        + [pltpu.VMEM((slots, PAIR), jnp.float32)] * 2,
        cost_estimate=pl.CostEstimate(
            flops=20 * half,
            bytes_accessed=14 * slots * columns,
            transcendentals=slots * slots * pairs,
        ),
        name="attention_grads",
    )(query, keys, values, mixed, grad, levels, lanes, rows)


ROW_BLOCK = 256


def whole_spec(array):
    zeros = (0,) * array.ndim
    return pl.BlockSpec(array.shape, lambda *_: zeros)


def row_spec(columns):
    return pl.BlockSpec((ROW_BLOCK, columns), lambda row, *_: (row, 0))


def own_spec(columns):
    return pl.BlockSpec((1, ROW_BLOCK, columns), lambda row, facts: (facts[0], row, 0))


def over_rows(kernel, slots, facts, inputs, outputs, flops):
    arrays, in_specs = zip(*inputs)
    shapes, out_specs = zip(*outputs)
    return pl.pallas_call(
        kernel,
        grid_spec=pltpu.PrefetchScalarGridSpec(
            num_scalar_prefetch=1,
            grid=(slots // ROW_BLOCK,),
            in_specs=list(in_specs),
            out_specs=list(out_specs),
        ),
        out_shape=list(shapes),
        cost_estimate=pl.CostEstimate(
            flops=flops,
            bytes_accessed=sum(array.size * array.dtype.itemsize for array in arrays),
            transcendentals=0,
        ),
    )(facts, *arrays)


def project_kernel(facts, tok_ref, gain_ref, shift_ref, w_ref, bias_ref, *refs):
    norm_ref, q_ref, k_ref, v_ref = refs[-4:]
    normal, _ = norm_parts(tok_ref[0].astype(jnp.float32))
    normed = (normal * gain_ref[...] + shift_ref[...]).astype(jnp.bfloat16)
    norm_ref[...] = normed
    q_ref[...] = (mm(normed, w_ref[0]) + bias_ref[0:1, :]).astype(jnp.bfloat16)
    k_ref[...] = mm(normed, w_ref[1]).astype(jnp.bfloat16)
    v_ref[...] = (mm(normed, w_ref[2]) + bias_ref[1:2, :]).astype(jnp.bfloat16)


def hidden_kernel(
    facts, tok_ref, a0_ref, a1_ref, w0_ref, w1_ref, bias_ref, gain_ref, shift_ref, hid_ref, norm_ref
):
    hidden = tok_ref[0].astype(jnp.float32) + bias_ref[...]
    hidden = hidden + mm(a0_ref[...], w0_ref[...]) + mm(a1_ref[...], w1_ref[...])
    hid_ref[...] = hidden
    normal, _ = norm_parts(hidden)
    norm_ref[...] = (normal * gain_ref[...] + shift_ref[...]).astype(jnp.bfloat16)


def act_kernel(norm_ref, w_ref, bias_ref, act_ref, slope_ref):
    def rows(number, carry):
        at = pl.ds(pl.multiple_of(number * ROW_BLOCK, ROW_BLOCK), ROW_BLOCK)
        value, slope = gelu_parts(mm(norm_ref[at, :], w_ref[...]) + bias_ref[...])
        act_ref[at, :] = value.astype(jnp.bfloat16)
        slope_ref[at, :] = slope.astype(jnp.bfloat16)
        return carry

    lax.fori_loop(0, norm_ref.shape[0] // ROW_BLOCK, rows, 0, unroll=True)


def activations(normed, weight, bias):
    slots, width = normed.shape
    hidden = weight.shape[1]
    columns = 512
    out = pl.BlockSpec((slots, columns), lambda col: (0, col))
    shape = jax.ShapeDtypeStruct((slots, hidden), jnp.bfloat16)
    return pl.pallas_call(
        act_kernel,
        grid=(hidden // columns,),
        in_specs=[
            whole_spec(normed),
            pl.BlockSpec((width, columns), lambda col: (0, col)),
            pl.BlockSpec((1, columns), lambda col: (0, col)),
        ],
        out_specs=(out, out),
        out_shape=(shape, shape),
        cost_estimate=pl.CostEstimate(
            flops=2 * slots * width * hidden,
            bytes_accessed=8 * slots * hidden,
            transcendentals=slots * hidden,
        ),
        name="activations",
    )(normed, weight, bias)


def output_kernel(facts, hid_ref, a0_ref, a1_ref, w0_ref, w1_ref, bias_ref, tie_ref, out_ref):
    total = hid_ref[...] + bias_ref[...] + mm(a0_ref[...], w0_ref[...])
    out_ref[...] = (total + mm(a1_ref[...], w1_ref[...])).astype(jnp.bfloat16)


def add_sums(sums_ref, rows):
    @pl.when(pl.program_id(0) == 0)
    def _():
        sums_ref[...] = jnp.zeros_like(sums_ref)

    for index, value in enumerate(rows):
        sums_ref[index : index + 1, :] += jnp.sum(value, 0, keepdims=True)


def hidden_grad_kernel(
    facts, g0_ref, g1_ref, w0_ref, w1_ref, hid_ref, gain_ref, dout_ref, grad_ref, one_ref, sums_ref
):
    grad_norm = mm(g0_ref[...], w0_ref[...], NT) + mm(g1_ref[...], w1_ref[...], NT)
    normal, inverse = norm_parts(hid_ref[...])
    place = lax.broadcasted_iota(jnp.int32, grad_norm.shape, 0) + pl.program_id(0) * ROW_BLOCK
    grad_out = jnp.where(place < facts[1], dout_ref[0].astype(jnp.float32), 0.0)
    grad = grad_out + norm_backward(grad_norm, normal, inverse, gain_ref[...])
    one = grad.astype(jnp.bfloat16)
    grad_ref[...] = grad
    one_ref[...] = one
    add_sums(sums_ref, [grad_norm * normal, grad_norm, one.astype(jnp.float32), grad_out])


def token_grad_kernel(
    facts, q0_ref, k0_ref, v0_ref, q1_ref, k1_ref, v1_ref, w0_ref, w1_ref, tok_ref, grad_ref,
    gain_ref, *refs,
):
    out_ref, sums_ref, heads_ref = refs[-3:]
    grad_norm = None
    for refs, weight in (((q0_ref, k0_ref, v0_ref), w0_ref), ((q1_ref, k1_ref, v1_ref), w1_ref)):
        for part, ref in enumerate(refs):
            more = mm(ref[...], weight[part], NT)
            grad_norm = more if grad_norm is None else grad_norm + more
    normal, inverse = norm_parts(tok_ref[0].astype(jnp.float32))
    grad = grad_ref[...] + norm_backward(grad_norm, normal, inverse, gain_ref[...])
    out_ref[...] = grad.astype(jnp.bfloat16)
    add_sums(sums_ref, [grad_norm * normal, grad_norm])
    add_sums(heads_ref, [ref[...].astype(jnp.float32) for ref in (q0_ref, q1_ref, v0_ref, v1_ref)])


RING = ((0, 0), (1, 0), (2, 0), (3, 0), (3, 1), (2, 1), (1, 1), (0, 1))


def device_of(z, y, core):
    return (z * 2 + y) * 2 + core


def to_tensor(value):
    return lax.ppermute(value, "tensor", [(0, 1), (1, 0)])


def to_core(value):
    return lax.ppermute(value, "dp", [(i, i ^ 1) for i in range(2 * len(RING))])


def rows_at(value, start, size):
    return lax.dynamic_slice_in_dim(value, start, size, value.ndim - 2)


def after(value, *earlier):
    return lax.optimization_barrier((value, *earlier))[0]


def piece(weight, index, pieces):
    size = weight.shape[-2] // pieces
    return rows_at(weight, index * size, size)


def both_cores(value, core, axis):
    beside = to_core(value)
    first = jnp.where(core == 0, value, beside)
    second = jnp.where(core == 0, beside, value)
    return jnp.concatenate([first, second], axis)


class Ring:
    def __init__(self, values, slots, sums, results, sems, cuts):
        self.values, self.slots, self.sums, self.results = values, slots, sums, results
        self.send_sems, self.recv_sems, self.swap_send_sems, self.swap_recv_sems = sems
        self.cuts = cuts
        self.count = count = len(RING)
        self.device = device = lax.axis_index("dp")
        self.core, self.y, self.z = lax.rem(device, 2), lax.rem(device // 2, 2), device // 4
        self.place = place = self.z * (1 - self.y) + (count - 1 - self.z) * self.y
        self.nexts = tuple(
            self.at_place(lax.rem(place + step, count)) for step in (1, count - 1)
        )
        self.partner = {"dp": device + 1 - 2 * self.core}
        self.streams = [
            (array, way, cut)
            for cut in range(cuts)
            for array in range(len(values))
            for way in range(2)
        ]

    def at_place(self, where):
        side = where // 4
        return {
            "dp": device_of(where * (1 - side) + (self.count - 1 - where) * side, side, self.core)
        }

    def greet(self, others=()):
        barrier = pltpu.get_barrier_semaphore()
        greeted = [*self.nexts, self.partner, *others]
        for target in greeted:
            pl.semaphore_signal(
                barrier, inc=1, device_id=target, device_id_type=pl.DeviceIdType.MESH
            )
        pl.semaphore_wait(barrier, len(greeted))

    def block(self, way, offset):
        return lax.rem(self.place - (1, -1)[way] * offset + 2 * self.count, self.count)

    def rows(self, array, cut):
        size = self.values[array].shape[2] // self.cuts
        return pl.ds(cut * size, size)

    def result(self, stream, step):
        array, way, cut = stream
        return self.results[array].at[
            self.core, way, self.block(way, step), self.rows(array, cut)
        ]

    def copy(self, stream, step):
        array, way, cut = stream
        rows = self.rows(array, cut)
        if step < self.count - 1:
            target = self.slots[array].at[way, step, rows]
            if step:
                source = self.sums[array].at[way, step - 1, rows]
            else:
                source = self.values[array].at[way, self.block(way, 0), rows]
        else:
            source = target = self.result(stream, step)
        index = self.streams.index(stream)
        return pltpu.make_async_remote_copy(
            src_ref=source,
            dst_ref=target,
            send_sem=self.send_sems.at[index, step],
            recv_sem=self.recv_sems.at[index, step],
            device_id=self.nexts[way],
            device_id_type=pl.DeviceIdType.MESH,
        )

    def swap(self, stream, step):
        index = self.streams.index(stream)
        turn = step - self.count + 1
        done = self.result(stream, step)
        return pltpu.make_async_remote_copy(
            src_ref=done,
            dst_ref=done,
            send_sem=self.swap_send_sems.at[index, turn],
            recv_sem=self.swap_recv_sems.at[index, turn],
            device_id=self.partner,
            device_id_type=pl.DeviceIdType.MESH,
        )

    def first(self):
        for stream in self.streams:
            self.copy(stream, 0).start()

    def hop(self, step):
        count = self.count
        for stream in self.streams:
            array, way, cut = stream
            rows = self.rows(array, cut)
            self.copy(stream, step - 1).wait_recv()
            if step < count:
                total = self.values[array][way, self.block(way, step), rows].astype(jnp.float32)
                total = total + self.slots[array][way, step - 1, rows].astype(jnp.float32)
                total = total.astype(jnp.bfloat16)
                if step < count - 1:
                    self.sums[array][way, step - 1, rows] = total
                else:
                    self.results[array][self.core, way, self.block(way, step), rows] = total
            self.copy(stream, step).start()
            if step >= count - 1:
                self.swap(stream, step).start()

    def last(self):
        for stream in self.streams:
            self.copy(stream, 2 * self.count - 3).wait_recv()
            self.swap(stream, 2 * self.count - 2).start()

    def drain(self):
        for stream in self.streams:
            for step in range(2 * self.count - 2):
                self.copy(stream, step).wait_send()
            for step in range(self.count - 1, 2 * self.count - 1):
                self.swap(stream, step).wait()


def ring_shape(value):
    count = len(RING)
    return value.reshape(2, count, value.shape[0] // (2 * count), value.shape[1])


def ring_scratch(shaped, cuts):
    count = len(RING)
    streams = 2 * len(shaped) * cuts
    scratch = [pltpu.VMEM((2, count - 1, *value.shape[2:]), value.dtype) for value in shaped]
    scratch += [pltpu.VMEM((2, count - 2, *value.shape[2:]), value.dtype) for value in shaped]
    scratch += [pltpu.SemaphoreType.DMA((streams, 2 * count - 2))] * 2
    return scratch + [pltpu.SemaphoreType.DMA((streams, count))] * 2


def ring_kernel(blocks, cuts, has_small, has_tie, *refs):
    values, refs = refs[:blocks], refs[blocks:]
    if has_small:
        small_ref, refs = refs[0], refs[1:]
    refs = refs[has_tie:]
    results, refs = refs[:blocks], refs[blocks:]
    if has_small:
        small_out, refs = refs[0], refs[1:]
    slots, refs = refs[:blocks], refs[blocks:]
    sums, refs = refs[:blocks], refs[blocks:]
    ring = Ring(values, slots, sums, results, refs[:4], cuts)
    if has_small:
        small_slots, small_sums, small_send_sems, small_recv_sems = refs[4:]
        device, y, z = ring.device, ring.y, ring.z
        small_targets = [
            ring.partner,
            {"tensor": 1 - lax.axis_index("tensor")},
            {"dp": device + 2 - 4 * y},
            {"dp": device + 4 - 8 * lax.rem(z, 2)},
            {"dp": device + 8 - 16 * (z // 2)},
        ]
        ring.greet(small_targets[1:])
    else:
        ring.greet()

    def exchange(turn):
        return pltpu.make_async_remote_copy(
            src_ref=small_ref if turn == 0 else small_sums.at[turn - 1],
            dst_ref=small_slots.at[turn],
            send_sem=small_send_sems.at[turn],
            recv_sem=small_recv_sems.at[turn],
            device_id=small_targets[turn],
            device_id_type=pl.DeviceIdType.MESH,
        )

    def take_exchange(turn):
        exchange(turn).wait_recv()
        total = (small_ref[...] if turn == 0 else small_sums[turn - 1]) + small_slots[turn]
        if turn == len(small_targets) - 1:
            small_out[...] = total
        else:
            small_sums[turn] = total
            exchange(turn + 1).start()

    ring.first()
    if has_small:
        exchange(0).start()
    for step in range(1, 2 * ring.count - 2):
        if has_small and step % 2 == 0 and step // 2 <= len(small_targets):
            take_exchange(step // 2 - 1)
        ring.hop(step)
    ring.last()
    ring.drain()
    if has_small:
        for turn in range(len(small_targets)):
            exchange(turn).wait_send()


def plane_sums(values, identity, small=None, tie=None, cuts=1):
    blocks = len(values)
    shaped = [ring_shape(value) for value in values]
    size = sum(value.size for value in values)
    vmem = pl.BlockSpec(memory_space=pltpu.VMEM)
    inputs, in_specs = list(shaped), [vmem] * blocks
    shapes = [jax.ShapeDtypeStruct((2, *value.shape), value.dtype) for value in shaped]
    scratch = ring_scratch(shaped, cuts)
    if small is not None:
        inputs.append(small)
        in_specs.append(vmem)
        shapes.append(jax.ShapeDtypeStruct(small.shape, small.dtype))
        scratch += [pltpu.VMEM((5, *small.shape), small.dtype)] * 2
        scratch += [pltpu.SemaphoreType.DMA((5,))] * 2
    if tie is not None:
        inputs.append(tie)
        in_specs.append(pl.BlockSpec(memory_space=pl.ANY))
    results = pl.pallas_call(
        functools.partial(ring_kernel, blocks, cuts, small is not None, int(tie is not None)),
        out_shape=shapes,
        in_specs=in_specs,
        out_specs=[vmem] * len(shapes),
        scratch_shapes=scratch,
        compiler_params=pltpu.CompilerParams(collective_id=identity, has_side_effects=True),
        cost_estimate=pl.CostEstimate(flops=size, bytes_accessed=6 * size, transcendentals=0),
        name="plane_sums",
    )(*inputs)
    sums = [
        result.reshape(2 * value.shape[0], value.shape[1]) for result, value in zip(results, values)
    ]
    return sums if small is None else (sums, results[-1])


def core_send(left, rights, core):
    half = left.shape[1] // 2
    part = lax.dynamic_slice_in_dim(left, (1 - core) * half, half, 1)
    sent = [contract_rows(part, right).astype(jnp.bfloat16) for right in rights]
    return sent, [to_core(value) for value in sent]


def core_sum(left, rights, arrived, core):
    half = left.shape[1] // 2
    kept = lax.dynamic_slice_in_dim(left, core * half, half, 1)
    return [
        contract_rows(kept, right) + part.astype(jnp.float32)
        for right, part in zip(rights, arrived)
    ]


def start_grad(left, rights, core):
    _, other = core_send(left[1], rights[1], core)
    sent, local = core_send(left[0], rights[0], core)
    summed = [part.astype(jnp.bfloat16) for part in core_sum(left[1], rights[1], other, core)]
    return local, [to_tensor(part) for part in summed], summed + sent


def pair_grad(left, rights, local, passed, core, *earlier):
    passed = [after(part, *earlier) for part in passed]
    return [
        (part + more.astype(jnp.float32)).astype(jnp.bfloat16)
        for part, more in zip(core_sum(left, rights, local, core), passed)
    ]


def trade_rows(value, own, *earlier):
    share = value.shape[0] // 2
    arrived = to_tensor(lax.dynamic_slice_in_dim(value, (1 - own) * share, share, 0))
    arrived = after(arrived, *earlier) if earlier else arrived
    kept = lax.dynamic_slice_in_dim(value, own * share, share, 0)
    return jnp.stack(
        [jnp.where(own == 0, kept, arrived), jnp.where(own == 0, arrived, kept)], 0
    )


def whole_sequence(*operands):
    return layer(*operands)


def layer(
    tokens,
    d_output,
    lengths,
    ln1_gain,
    ln1_bias,
    w_qkv,
    qv_bias,
    w_out,
    bias_out,
    ln2_gain,
    ln2_bias,
    w_up,
    b_up,
    w_down,
    b_down,
):
    own = lax.axis_index("tensor")
    device = lax.axis_index("dp")
    core = device % 2
    slots, width = tokens.shape[1:]
    local_width = w_qkv.shape[2]
    hidden_local = w_up.shape[1]
    table = jnp.asarray(slope_rows())
    pairs = local_width // PAIR
    f32 = jnp.float32

    weight_qkv = w_qkv.transpose(1, 0, 2)
    biases = jnp.concatenate([qv_bias.reshape(-1), b_up])
    other_biases = to_tensor(biases)
    piece_up, piece_qkv = piece(w_up, device, 2 * len(RING)), piece(weight_qkv, core, 2)
    far_up = to_tensor(piece_up)
    far_qkv = to_tensor(piece_qkv)
    qv = [b[: 2 * local_width].reshape(2, local_width).astype(f32) for b in (biases, other_biases)]
    ups = [b[2 * local_width :].astype(f32)[None] for b in (biases, other_biases)]
    rows = [lax.dynamic_slice_in_dim(table, index * pairs, pairs, 0) for index in (own, 1 - own)]
    gain_one, shift_one = ln1_gain.astype(f32)[None], ln1_bias.astype(f32)[None]
    gain_two, shift_two = ln2_gain.astype(f32)[None], ln2_bias.astype(f32)[None]

    length = lax.dynamic_index_in_dim(lengths, own, 0, keepdims=False)
    facts = jnp.stack([own.astype(jnp.int32), length])
    lanes = key_lanes(slots, length)
    low = jnp.bfloat16

    def run(kernel, inputs, outputs, flops):
        return over_rows(kernel, slots, facts, inputs, outputs, flops)

    def fixed(array):
        return array, whole_spec(array)

    def tied(array):
        return array, pl.BlockSpec(memory_space=pl.ANY)

    def by_row(array):
        return array, row_spec(array.shape[1])

    def rows_out(columns, dtype):
        return jax.ShapeDtypeStruct((slots, columns), dtype), row_spec(columns)

    def sums_out(columns):
        shape = jax.ShapeDtypeStruct((8, columns), f32)
        return shape, whole_spec(shape)

    square = 2 * slots * width
    tokens_in, d_output_in = (tokens, own_spec(width)), (d_output, own_spec(width))
    normed_one, *local_heads = run(
        project_kernel,
        [tokens_in, fixed(gain_one), fixed(shift_one), fixed(weight_qkv), fixed(qv[0])]
        + [tied(piece_up), tied(piece_qkv)],
        [rows_out(width, low)] + [rows_out(local_width, low)] * 3,
        3 * square * local_width,
    )
    attn, level = attention_out(*local_heads, lanes, rows[0])
    heads, mixed, levels = [tuple(local_heads)], [attn], [level]
    far_out = to_tensor(after(piece(w_out, core, 2), normed_one))
    far_down = to_tensor(after(piece(w_down, device, 2 * len(RING)), normed_one))
    up = (w_up, lax.all_gather(after(far_up, normed_one), "dp", axis=0, tiled=True))
    qkv = (weight_qkv, both_cores(after(far_qkv, attn), core, 1))
    query = (matmul(normed_one, qkv[1][0]) + qv[1][0]).astype(low)
    keys = matmul(normed_one, qkv[1][1]).astype(low)
    values = (matmul(normed_one, qkv[1][2]) + qv[1][1]).astype(low)
    heads.append((query, keys, values))
    out = (w_out, both_cores(after(far_out, keys), core, 0))
    attn, level = attention_out(query, keys, values, lanes, rows[1])
    mixed.append(attn)
    levels.append(level)
    down = (w_down, lax.all_gather(after(far_down, attn), "dp", axis=0, tiled=True))
    hidden, normed_two = run(
        hidden_kernel,
        [tokens_in, by_row(mixed[0]), by_row(mixed[1]), fixed(out[0]), fixed(out[1])]
        + [fixed(bias_out.astype(f32)[None]), fixed(gain_two), fixed(shift_two)],
        [rows_out(width, f32), rows_out(width, low)],
        2 * square * local_width,
    )
    acts = [activations(normed_two, up[0], ups[0])]
    up = (up[0], after(up[1], acts[0][0]))
    acts.append(activations(normed_two, up[1], ups[1]))

    valid = (jnp.arange(slots, dtype=jnp.int32) < length).astype(f32)[:, None]
    grad_out = lax.dynamic_index_in_dim(d_output, own, 0, keepdims=False).astype(f32) * valid
    grad_two = grad_out.astype(low)
    left_down, right_down = (acts[0][0], acts[1][0]), ([grad_two], [grad_two])
    local_down, passed_down, sent = start_grad(left_down, right_down, core)
    late_two = after(grad_two, *sent)

    bias_up = []

    def pre_grad(weight, slope):
        value = (contract_cols(late_two, weight) * slope.astype(f32)).astype(low)
        bias_up.append(jnp.sum(value.astype(f32), 0))
        return value

    grad_pre = [pre_grad(down[0], acts[0][1])]
    down = (down[0], after(down[1], grad_pre[0]))
    grad_pre.append(pre_grad(down[1], acts[1][1]))
    left_up, right_up = (normed_two, normed_two), ([grad_pre[0]], [grad_pre[1]])
    local_up, passed_up, sent = start_grad(left_up, right_up, core)
    late_pre = lax.optimization_barrier((*grad_pre, *sent))
    grad_hidden, grad_one, sums_two = run(
        hidden_grad_kernel,
        [by_row(late_pre[0]), by_row(late_pre[1]), fixed(up[0]), fixed(up[1]), by_row(hidden)]
        + [fixed(gain_two), d_output_in],
        [rows_out(width, f32), rows_out(width, low), sums_out(width)],
        2 * square * hidden_local,
    )
    left_out, right_out = (mixed[0], mixed[1]), ([grad_one], [grad_one])
    local_out, passed_out, sent = start_grad(left_out, right_out, core)
    (result,) = run(
        output_kernel,
        [by_row(hidden), by_row(acts[0][0]), by_row(acts[1][0]), fixed(down[0]), fixed(down[1])]
        + [fixed(b_down.astype(f32)[None]), tied(sent[0])],
        [rows_out(width, low)],
        2 * square * hidden_local,
    )
    late_one = after(grad_one, *sent, result)
    grads = [None, None]
    grad_attn = contract_cols(late_one, out[1]).astype(low)
    grads[1] = attention_grads(*heads[1], mixed[1], levels[1], grad_attn, lanes, rows[1])
    _, other_qkv = core_send(normed_one, grads[1], core)
    sent_qkv = [part.astype(low) for part in core_sum(normed_one, grads[1], other_qkv, core)]
    passed_qkv = [to_tensor(part) for part in sent_qkv]
    later_one = after(late_one, *sent_qkv)
    grad_attn = contract_cols(later_one, out[0]).astype(low)
    grads[0] = attention_grads(*heads[0], mixed[0], levels[0], grad_attn, lanes, rows[0])
    sent, local_qkv = core_send(normed_one, grads[0], core)
    grad_tokens, sums_one, sums_heads = run(
        token_grad_kernel,
        [by_row(part) for part in (*grads[0], *grads[1])]
        + [fixed(qkv[0]), fixed(qkv[1]), tokens_in, by_row(grad_hidden), fixed(gain_one)]
        + [tied(part) for part in sent],
        [rows_out(width, low), sums_out(width), sums_out(local_width)],
        6 * square * local_width,
    )
    done = grad_tokens
    output, grad_tokens = trade_rows(result, own, done), trade_rows(grad_tokens, own)

    def in_place(first, second):
        return jnp.concatenate(
            [jnp.where(own == 0, first, second), jnp.where(own == 0, second, first)], 0
        )

    small = jnp.concatenate(
        [
            sums_one[:2],
            sums_two[:4],
            in_place(sums_heads[0], sums_heads[1]).reshape(1, width),
            in_place(sums_heads[2], sums_heads[3]).reshape(1, width),
            in_place(*bias_up).reshape(-1, width),
        ],
        0,
    )
    small = jnp.pad(small, ((0, 16 - small.shape[0]), (0, 0)))
    mine = [
        *pair_grad(left_down[0], right_down[0], local_down, passed_down, core, done),
        *pair_grad(left_up[0], right_up[0], local_up, passed_up, core, done),
        *pair_grad(left_out[0], right_out[0], local_out, passed_out, core, done),
        *pair_grad(normed_one, grads[0], local_qkv, passed_qkv, core, done),
    ]
    (grad_wdown, grad_wup, grad_wout, *grad_wqkv), small = plane_sums(mine, 1, small)
    grad_wqkv = jnp.stack(grad_wqkv, 0).astype(f32)
    wide = [lax.dynamic_slice_in_dim(small[i], own * local_width, local_width, 0) for i in (6, 7)]
    grad_bup = lax.dynamic_slice_in_dim(
        small[8:12].reshape(-1), own * hidden_local, hidden_local, 0
    )
    return (
        output,
        grad_tokens,
        small[0],
        small[1],
        grad_wqkv.transpose(1, 0, 2),
        jnp.stack(wide, 0),
        grad_wout.astype(f32),
        small[4],
        small[2],
        small[3],
        grad_wup.astype(f32),
        grad_bup,
        grad_wdown.astype(f32),
        small[5],
    )


def on_device(
    tokens,
    d_output,
    lengths,
    ln1_gain,
    ln1_bias,
    w_qkv,
    qv_bias,
    w_out,
    bias_out,
    ln2_gain,
    ln2_bias,
    w_up,
    b_up,
    w_down,
    b_down,
):
    parts = lax.axis_size("tensor")
    place = lax.axis_index("tensor")
    batches, slots, width = tokens.shape
    share = slots // parts
    row_start = place * share
    local_width = w_qkv.shape[2]
    hidden_local = w_up.shape[1]
    heads_local = local_width // HEAD_DIM
    scale = 1.0 / math.sqrt(HEAD_DIM)
    first_head = place * heads_local
    slopes = jnp.exp2(
        -8.0
        * ((first_head + jnp.arange(heads_local, dtype=jnp.int32)).astype(jnp.float32) + 1.0)
        / HEADS
    )
    weight_qkv = w_qkv.reshape(width, 3 * local_width)
    qkv_shift = jnp.concatenate(
        [
            qv_bias[0].astype(jnp.float32),
            jnp.zeros((local_width,), jnp.float32),
            qv_bias[1].astype(jnp.float32),
        ]
    )
    gain_one = ln1_gain.astype(jnp.float32)
    shift_one = ln1_bias.astype(jnp.float32)
    gain_two = ln2_gain.astype(jnp.float32)
    shift_two = ln2_bias.astype(jnp.float32)
    out_shift = bias_out.astype(jnp.float32)
    up_shift = b_up.astype(jnp.float32)
    down_shift = b_down.astype(jnp.float32)
    grad_qkv = jnp.zeros((width, 3 * local_width), jnp.float32)
    grad_qvb = jnp.zeros((2, local_width), jnp.float32)
    grad_wout = jnp.zeros((local_width, width), jnp.float32)
    grad_wup = jnp.zeros((width, hidden_local), jnp.float32)
    grad_bup = jnp.zeros((hidden_local,), jnp.float32)
    grad_wdown = jnp.zeros((hidden_local, width), jnp.float32)
    grad_gain_one = jnp.zeros((width,), jnp.float32)
    grad_shift_one = jnp.zeros((width,), jnp.float32)
    grad_gain_two = jnp.zeros((width,), jnp.float32)
    grad_shift_two = jnp.zeros((width,), jnp.float32)
    grad_out_shift = jnp.zeros((width,), jnp.float32)
    grad_down_shift = jnp.zeros((width,), jnp.float32)
    output_rows = []
    input_rows = []
    for index in range(batches):
        tokens_f = tokens[index].astype(jnp.float32)
        length = lengths[index]
        normal_one, inverse_one = norm_parts(tokens_f)
        normed_one = (normal_one * gain_one + shift_one).astype(jnp.bfloat16)
        projected = (matmul(normed_one, weight_qkv) + qkv_shift).astype(jnp.bfloat16)
        query = projected[:, :local_width].reshape(slots, heads_local, HEAD_DIM)
        keys = projected[:, local_width : 2 * local_width].reshape(slots, heads_local, HEAD_DIM)
        values = projected[:, 2 * local_width :].reshape(slots, heads_local, HEAD_DIM)
        attn = attention_forward(query, keys, values, length, slopes, scale)
        partial_value = matmul(attn, w_out)
        summed = lax.psum(partial_value.astype(jnp.bfloat16), "tensor").astype(jnp.float32)
        hidden_full = tokens_f + summed + out_shift
        normal_full, inverse_full = norm_parts(hidden_full)
        normed_two = (normal_full * gain_two + shift_two).astype(jnp.bfloat16)
        hidden_rows = lax.dynamic_slice_in_dim(hidden_full, row_start, share, 0)
        normal_two = lax.dynamic_slice_in_dim(normal_full, row_start, share, 0)
        inverse_two = lax.dynamic_slice_in_dim(inverse_full, row_start, share, 0)
        pre = matmul(normed_two, w_up) + up_shift
        act_value, act_slope = gelu_parts(pre)
        act = act_value.astype(jnp.bfloat16)
        mlp_part = lax.psum_scatter(
            matmul(act, w_down).astype(jnp.bfloat16), "tensor", scatter_dimension=0, tiled=True
        ).astype(jnp.float32)
        output_rows.append((hidden_rows + mlp_part + down_shift).astype(jnp.bfloat16))
        valid = (jnp.arange(slots, dtype=jnp.int32) < length).astype(jnp.float32)[:, None]
        grad_out = d_output[index].astype(jnp.float32) * valid
        grad_two = grad_out.astype(jnp.bfloat16)
        grad_wdown = grad_wdown + contract_rows(act, grad_two)
        grad_pre = (contract_cols(grad_two, w_down) * act_slope).astype(jnp.bfloat16)
        grad_wup = grad_wup + contract_rows(normed_two, grad_pre)
        grad_bup = grad_bup + jnp.sum(grad_pre.astype(jnp.float32), 0)
        grad_norm_two = lax.psum_scatter(
            contract_cols(grad_pre, w_up).astype(jnp.bfloat16),
            "tensor",
            scatter_dimension=0,
            tiled=True,
        ).astype(jnp.float32)
        grad_gain_two = grad_gain_two + jnp.sum(grad_norm_two * normal_two, 0)
        grad_shift_two = grad_shift_two + jnp.sum(grad_norm_two, 0)
        grad_out_rows = lax.dynamic_slice_in_dim(grad_out, row_start, share, 0)
        grad_hidden_rows = grad_out_rows + norm_backward(
            grad_norm_two, normal_two, inverse_two, gain_two
        )
        grad_one_rows = grad_hidden_rows.astype(jnp.bfloat16)
        grad_down_shift = grad_down_shift + jnp.sum(
            lax.dynamic_slice_in_dim(grad_two, row_start, share, 0).astype(jnp.float32), 0
        )
        grad_out_shift = grad_out_shift + jnp.sum(grad_one_rows.astype(jnp.float32), 0)
        grad_one = lax.all_gather(grad_one_rows, "tensor", axis=0, tiled=True)
        grad_wout = grad_wout + contract_rows(attn, grad_one)
        grad_attn = (
            contract_cols(grad_one, w_out)
            .astype(jnp.bfloat16)
            .reshape(slots, heads_local, HEAD_DIM)
        )
        grad_query, grad_keys, grad_values = attention_backward(
            query, keys, values, grad_attn, length, slopes, scale
        )
        grad_proj = jnp.concatenate([grad_query, grad_keys, grad_values], 1)
        grad_qkv = grad_qkv + contract_rows(normed_one, grad_proj)
        grad_qvb = grad_qvb + jnp.stack(
            [
                jnp.sum(grad_query.astype(jnp.float32), 0),
                jnp.sum(grad_values.astype(jnp.float32), 0),
            ],
            0,
        )
        grad_norm_one = lax.psum_scatter(
            contract_cols(grad_proj, weight_qkv).astype(jnp.bfloat16),
            "tensor",
            scatter_dimension=0,
            tiled=True,
        ).astype(jnp.float32)
        normal_one_rows = lax.dynamic_slice_in_dim(normal_one, row_start, share, 0)
        inverse_one_rows = lax.dynamic_slice_in_dim(inverse_one, row_start, share, 0)
        grad_gain_one = grad_gain_one + jnp.sum(grad_norm_one * normal_one_rows, 0)
        grad_shift_one = grad_shift_one + jnp.sum(grad_norm_one, 0)
        input_rows.append(
            (
                grad_hidden_rows
                + norm_backward(grad_norm_one, normal_one_rows, inverse_one_rows, gain_one)
            ).astype(jnp.bfloat16)
        )
    grad_qkv, grad_qvb, grad_wout, grad_wup, grad_bup, grad_wdown = (
        lax.psum(grad_qkv.astype(jnp.bfloat16), "dp").astype(jnp.float32),
        lax.psum(grad_qvb.astype(jnp.bfloat16), "dp").astype(jnp.float32),
        lax.psum(grad_wout.astype(jnp.bfloat16), "dp").astype(jnp.float32),
        lax.psum(grad_wup.astype(jnp.bfloat16), "dp").astype(jnp.float32),
        lax.psum(grad_bup.astype(jnp.bfloat16), "dp").astype(jnp.float32),
        lax.psum(grad_wdown.astype(jnp.bfloat16), "dp").astype(jnp.float32),
    )
    (
        grad_gain_one,
        grad_shift_one,
        grad_gain_two,
        grad_shift_two,
        grad_out_shift,
        grad_down_shift,
    ) = lax.psum(
        (
            grad_gain_one,
            grad_shift_one,
            grad_gain_two,
            grad_shift_two,
            grad_out_shift,
            grad_down_shift,
        ),
        ("dp", "tensor"),
    )
    return (
        jnp.stack(output_rows, 0),
        jnp.stack(input_rows, 0),
        grad_gain_one,
        grad_shift_one,
        grad_qkv.reshape(width, 3, local_width),
        grad_qvb,
        grad_wout,
        grad_out_shift,
        grad_gain_two,
        grad_shift_two,
        grad_wup,
        grad_bup,
        grad_wdown,
        grad_down_shift,
    )


def solution(mesh):
    whole = mesh.shape["tensor"] == 2 and mesh.shape["dp"] == 2 * len(RING)
    return jax.shard_map(
        whole_sequence if whole else on_device,
        mesh=mesh,
        in_specs=(
            P("dp", None, None),
            P("dp", None, None),
            P("dp"),
            P(),
            P(),
            P(None, None, "tensor"),
            P(None, "tensor"),
            P("tensor", None),
            P(),
            P(),
            P(),
            P(None, "tensor"),
            P("tensor"),
            P("tensor", None),
            P(),
        ),
        out_specs=(
            P("dp", "tensor", None),
            P("dp", "tensor", None),
            P(),
            P(),
            P(None, None, "tensor"),
            P(None, "tensor"),
            P("tensor", None),
            P(),
            P(),
            P(),
            P(None, "tensor"),
            P("tensor"),
            P("tensor", None),
            P(),
        ),
        check_vma=False,
    )
```

profile of v0, /device:TPU:0, one launch (start us, length us, event | category | flops | bytes accessed | tf_op | source)
XLA Modules:
  0.0 593.3 jit_solution(4883990921416175214)
XLA Ops:
  20.2 8.8 %shard_map.263 = (bf16[1024,1024]{1,0:T(8,128)(2,1)}, bf16[1024,512]{1,0:T(8,128)(2,1)}, bf16[1024,512]{1,0:T(8,128)(2,1)}, bf16[1024,512]{1,0:T(8,128)(2,1)}) custom-call(s32[2]{0:T(128)} %pad_add_fusion.facts, bf16[2,1024,1024]{2,1,0:T(8,128)(2,1)} %tok_ref.5, f32[1,1024]{1,0:T(1,128)} %bitcast.142, f32[1,1024]{1,0:T(1,128)} %bitcast.145, ...), custom_call_target="tpu_custom_call" | custom-call | flops 3221225472 | bytes 9187328 | tf_op jit(solution)/shard_map/pallas_call | solution.py:360
  32.4 12.9 %attention_out.2 = (bf16[1024,512]{1,0:T(8,128)(2,1)}, f32[4,8,1024]{2,1,0:T(8,128)}) custom-call(bf16[1024,512]{1,0:T(8,128)(2,1)} %get-tuple-element.67.q_ref, bf16[1024,512]{1,0:T(8,128)(2,1)} %get-tuple-element.68.k_ref, bf16[1024,512]{1,0:T(8,128)(2,1)} %get-tuple-element.69.v_ref, bf16[1024,128]{1,0:T(8,128)(2,1)} %select_convert_fusion.lanes_ref, ...), custom_call_target="tpu_custom_call" | custom-call | flops 4294967296 | bytes 4194304 | tf_op jit(solution)/shard_map/attention_out/pallas_call | solution.py:300
  45.2 20.4 %collective-permute-done = bf16[3,512,512]{2,1,0:T(8,128)(2,1)S(1)} collective-permute-done((bf16[3,512,512]{2,1,0:T(8,128)(2,1)S(1)}, bf16[3,512,512]{2,1,0:T(8,128)(2,1)S(1)}, u32[]{:S(2)}, u32[]{:S(2)}) %collective-permute-start) | collective-permute-done | bytes 1572896 | tf_op jit(solution)/shard_map/ppermute | solution.py:486
  78.8 13.0 %attention_out.3 = (bf16[1024,512]{1,0:T(8,128)(2,1)}, f32[4,8,1024]{2,1,0:T(8,128)}) custom-call(bf16[1024,512]{1,0:T(8,128)(2,1)} %add_convert_fusion.5.q_ref, bf16[1024,512]{1,0:T(8,128)(2,1)} %convolution_convert_fusion.4.k_ref, bf16[1024,512]{1,0:T(8,128)(2,1)} %add_convert_fusion.4.v_ref, bf16[1024,128]{1,0:T(8,128)(2,1)} %select_convert_fusion.lanes_ref, ...), custom_call_target="tpu_custom_call" | custom-call | flops 4294967296 | bytes 4194304 | tf_op jit(solution)/shard_map/attention_out/pallas_call | solution.py:300
  92.3 13.3 %collective-permute-done.3 = bf16[256,1024]{1,0:T(8,128)(2,1)S(1)} collective-permute-done((bf16[256,1024]{1,0:T(8,128)(2,1)S(1)}, bf16[256,1024]{1,0:T(8,128)(2,1)S(1)}, u32[]{:S(2)}, u32[]{:S(2)}) %collective-permute-start.3) | collective-permute-done | bytes 524320 | tf_op jit(solution)/shard_map/ppermute | solution.py:486
  114.4 8.3 %shard_map.264 = (f32[1024,1024]{1,0:T(8,128)}, bf16[1024,1024]{1,0:T(8,128)(2,1)}) custom-call(s32[2]{0:T(128)} %pad_add_fusion.facts, bf16[2,1024,1024]{2,1,0:T(8,128)(2,1)} %tok_ref.5, bf16[1024,512]{1,0:T(8,128)(2,1)} %get-tuple-element.70.a0_ref.o_ref, bf16[1024,512]{1,0:T(8,128)(2,1)} %get-tuple-element.73.a1_ref.o_ref, bf16[512,1024]{1,0:T(8,128)(2,1)} %w0_ref.3, ...), custom_call_target="tpu_custom_call" | custom-call | flops 2147483648 | bytes 8400896 | tf_op jit(solution)/shard_map/pallas_call | solution.py:360
  122.8 13.5 %activations.2 = (bf16[1024,2048]{1,0:T(8,128)(2,1)}, bf16[1024,2048]{1,0:T(8,128)(2,1)}) custom-call(bf16[1024,1024]{1,0:T(8,128)(2,1)} %get-tuple-element.77.norm_ref, bf16[1024,2048]{1,0:T(8,128)(2,1)} %w0_ref.4, f32[1,2048]{1,0:T(1,128)} %bitcast.129), custom_call_target="tpu_custom_call" | custom-call | flops 4294967296 | bytes 16777216 | tf_op jit(solution)/shard_map/activations/pallas_call | solution.py:414
  136.3 13.4 %activations.3 = (bf16[1024,2048]{1,0:T(8,128)(2,1)}, bf16[1024,2048]{1,0:T(8,128)(2,1)}) custom-call(bf16[1024,1024]{1,0:T(8,128)(2,1)} %get-tuple-element.77.norm_ref, bf16[1024,2048]{1,0:T(8,128)(2,1)} %all-gather.3.cloned.1.call-done.w_ref.w1_ref, f32[1,2048]{1,0:T(1,128)} %bitcast.130), custom_call_target="tpu_custom_call" | custom-call | flops 4294967296 | bytes 16777216 | tf_op jit(solution)/shard_map/activations/pallas_call | solution.py:414
  149.7 5.9 fusion.9
  156.2 6.1 %fusion.12 = bf16[1024,1024]{1,0:T(8,128)(2,1)} fusion(bf16[1024,1024]{1,0:T(8,128)(2,1)} %fusion, bf16[1024,2048]{1,0:T(8,128)(2,1)} %get-tuple-element.78.a0_ref, s32[]{:T(128)S(6)} %select_n.250), kind=kOutput, calls=%fused_computation.35 | convolution fusion | flops 2148532224 | bytes 6291460 | tf_op jit(solution)/shard_map/dot_general | solution.py:26
  162.4 5.6 add_convert_fusion.3
  168.0 6.1 %convert_reduce_fusion.1 = (f32[2048]{0:T(1024)S(1)}, bf16[1024,2048]{1,0:T(8,128)(2,1)}) fusion(bf16[1024,2048]{1,0:T(8,128)(2,1)S(1)} %copy-done.56, bf16[1024,1024]{1,0:T(8,128)(2,1)S(1)} %copy-done.12, bf16[2048,1024]{1,0:T(8,128)(2,1)S(1)} %copy-done.31), kind=kOutput, calls=%fused_computation.1 | convolution fusion | flops 4305451008 | bytes 14688256 | tf_op jit(solution)/shard_map/dot_general | solution.py:32
  174.1 7.2 %fusion.112 = f32[1024,2048]{1,0:T(8,128)S(1)} fusion(bf16[1024,1024]{1,0:T(8,128)(2,1)} %fusion, bf16[2048,1024]{1,0:T(8,128)(2,1)} %all-gather.5.cloned.1.call-done.w1_ref), kind=kOutput, calls=%fused_computation.178 | convolution fusion | flops 4294967296 | bytes 14680064 | tf_op jit(solution)/shard_map/dot_general | solution.py:32
  185.1 5.7 convolution_convert_fusion.1
  195.9 4.4 fusion.1
  200.6 3.9 convolution_convert_fusion
  204.7 4.5 fusion.34
  209.2 7.0 %add_convert_fusion.2 = bf16[512,2048]{1,0:T(8,128)(2,1)} fusion(bf16[512,2048]{1,0:T(8,128)(2,1)} %collective-permute-done.8, bf16[1024,2048]{1,0:T(8,128)(2,1)} %copy-done.1, bf16[1024,1024]{1,0:T(8,128)(2,1)S(1)} %copy-done.27, s32[]{:T(128)S(6)} %select_n.231), kind=kOutput, calls=%fused_computation.18 | convolution fusion | flops 2150629376 | bytes 9437188 | tf_op jit(solution)/shard_map/dot_general | solution.py:26
  216.2 18.8 %shard_map.265 = (f32[1024,1024]{1,0:T(8,128)}, bf16[1024,1024]{1,0:T(8,128)(2,1)}, f32[8,1024]{1,0:T(8,128)}) custom-call(s32[2]{0:T(128)} %pad_add_fusion.facts, bf16[1024,2048]{1,0:T(8,128)(2,1)} %get-tuple-element.88.g0_ref, bf16[1024,2048]{1,0:T(8,128)(2,1)} %copy-done.1, bf16[1024,2048]{1,0:T(8,128)(2,1)} %w0_ref.4, ...), custom_call_target="tpu_custom_call" | custom-call | flops 8589934592 | bytes 25169920 | tf_op jit(solution)/shard_map/pallas_call | solution.py:360
  243.7 15.7 %shard_map.266 = bf16[1024,1024]{1,0:T(8,128)(2,1)} custom-call(s32[2]{0:T(128)} %pad_add_fusion.facts, f32[1024,1024]{1,0:T(8,128)} %get-tuple-element.76.hid_ref, bf16[1024,2048]{1,0:T(8,128)(2,1)} %get-tuple-element.78.a0_ref, bf16[1024,2048]{1,0:T(8,128)(2,1)} %get-tuple-element.81.a1_ref, bf16[2048,1024]{1,0:T(8,128)(2,1)} %w0_ref.5, ...), custom_call_target="tpu_custom_call" | custom-call | flops 8589934592 | bytes 21499904 | tf_op jit(solution)/shard_map/pallas_call | solution.py:360
  261.7 19.9 %attention_grads.2 = (bf16[1024,512]{1,0:T(8,128)(2,1)}, bf16[1024,512]{1,0:T(8,128)(2,1)}, bf16[1024,512]{1,0:T(8,128)(2,1)}) custom-call(bf16[1024,512]{1,0:T(8,128)(2,1)} %add_convert_fusion.5.q_ref, bf16[1024,512]{1,0:T(8,128)(2,1)} %convolution_convert_fusion.4.k_ref, bf16[1024,512]{1,0:T(8,128)(2,1)} %add_convert_fusion.4.v_ref, ...), custom_call_target="tpu_custom_call" | custom-call | flops 10737418240 | bytes 7340032 | tf_op jit(solution)/shard_map/attention_grads/pallas_call | solution.py:324
  297.0 20.0 %attention_grads.3 = (bf16[1024,512]{1,0:T(8,128)(2,1)}, bf16[1024,512]{1,0:T(8,128)(2,1)}, bf16[1024,512]{1,0:T(8,128)(2,1)}) custom-call(bf16[1024,512]{1,0:T(8,128)(2,1)} %get-tuple-element.67.q_ref, bf16[1024,512]{1,0:T(8,128)(2,1)} %get-tuple-element.68.k_ref, bf16[1024,512]{1,0:T(8,128)(2,1)} %get-tuple-element.69.v_ref, ...), custom_call_target="tpu_custom_call" | custom-call | flops 10737418240 | bytes 7340032 | tf_op jit(solution)/shard_map/attention_grads/pallas_call | solution.py:324
  323.0 15.9 %shard_map.267 = (bf16[1024,1024]{1,0:T(8,128)(2,1)}, f32[8,1024]{1,0:T(8,128)}, f32[8,512]{1,0:T(8,128)}) custom-call(s32[2]{0:T(128)} %pad_add_fusion.facts, bf16[1024,512]{1,0:T(8,128)(2,1)} %get-tuple-element.98.q0_ref, bf16[1024,512]{1,0:T(8,128)(2,1)} %get-tuple-element.99.k0_ref, bf16[1024,512]{1,0:T(8,128)(2,1)} %get-tuple-element.100.v0_ref, ...), custom_call_target="tpu_custom_call" | custom-call | flops 6442450944 | bytes 22548480 | tf_op jit(solution)/shard_map/pallas_call | solution.py:360
  342.9 6.0 %add_convert_fusion.1 = bf16[1024,1024]{1,0:T(8,128)(2,1)} fusion(bf16[1024,1024]{1,0:T(8,128)(2,1)} %collective-permute-done.16, f32[1024,1024]{1,0:T(8,128)} %fusion.1, bf16[1024,1024]{1,0:T(8,128)(2,1)} %collective-permute-done.15), kind=kLoop, calls=%fused_computation.17 | loop fusion | flops 5242880 | bytes 10485760 | tf_op jit(solution)/shard_map/convert_element_type | solution.py:761
  357.6 18.9 %collective-permute-done.10 = bf16[512,1024]{1,0:T(8,128)(2,1)S(1)} collective-permute-done((bf16[512,1024]{1,0:T(8,128)(2,1)S(1)}, bf16[512,1024]{1,0:T(8,128)(2,1)S(1)}, u32[]{:S(2)}, u32[]{:S(2)}) %collective-permute-start.10) | collective-permute-done | bytes 1048608 | tf_op jit(solution)/shard_map/ppermute | solution.py:486
  376.8 11.1 %collective-permute-done.22 = bf16[512,512]{1,0:T(8,128)(2,1)} collective-permute-done((bf16[512,512]{1,0:T(8,128)(2,1)S(1)}, bf16[512,512]{1,0:T(8,128)(2,1)}, u32[]{:S(2)}, u32[]{:S(2)}) %collective-permute-start.22) | collective-permute-done | bytes 524320 | tf_op jit(solution)/shard_map/ppermute | solution.py:486
  389.3 9.8 %collective-permute-done.24 = bf16[512,512]{1,0:T(8,128)(2,1)} collective-permute-done((bf16[512,512]{1,0:T(8,128)(2,1)}, bf16[512,512]{1,0:T(8,128)(2,1)}, u32[]{:S(2)}, u32[]{:S(2)}) %collective-permute-start.24) | collective-permute-done | bytes 524320 | tf_op jit(solution)/shard_map/ppermute | solution.py:486
  400.9 8.9 %collective-permute-done.26 = bf16[512,512]{1,0:T(8,128)(2,1)} collective-permute-done((bf16[512,512]{1,0:T(8,128)(2,1)}, bf16[512,512]{1,0:T(8,128)(2,1)}, u32[]{:S(2)}, u32[]{:S(2)}) %collective-permute-start.26) | collective-permute-done | bytes 524320 | tf_op jit(solution)/shard_map/ppermute | solution.py:486
  418.2 4.7 add_convert_fusion
  423.0 138.8 %plane_sums.1 = (bf16[2,2,8,64,1024]{4,3,2,1,0:T(8,128)(2,1)}, bf16[2,2,8,32,2048]{4,3,2,1,0:T(8,128)(2,1)}, bf16[2,2,8,16,1024]{4,3,2,1,0:T(8,128)(2,1)}, bf16[...) custom-call(bf16[2,8,64,1024]{3,2,1,0:T(8,128)(2,1)} %bitcast.110, ...), custom_call_target="tpu_custom_call" | custom-call | flops 3145728 | bytes 18874368 | tf_op jit(solution)/shard_map/plane_sums/pallas_call | solution.py:719
  567.2 6.8 %bitcast_convert_fusion.1 = f32[1024,2048]{1,0:T(8,128)} fusion(bf16[2,2,8,32,2048]{4,3,2,1,0:T(8,128)(2,1)} %get-tuple-element.118), kind=kLoop, calls=%fused_computation.13 | loop fusion | flops 2097152 | bytes 12582912 | tf_op jit(solution)/shard_map/convert_element_type | solution.py:975
  579.3 4.7 bitcast_convert_fusion
  (250 shorter events, 118.1 us)
Async XLA Ops:
  7.2 129.1 %all-gather.3.cloned.1.call-start = ((), (), s32[]{:S(2)}) async-start(), calls=%async_computation | async-start | bytes 4456448 | tf_op jit(solution)/shard_map/all_gather | solution.py:856
  8.2 20.8 %collective-permute-start.5 = (bf16[64,2048]{1,0:T(8,128)(2,1)S(1)}, bf16[64,2048]{1,0:T(8,128)(2,1)S(1)}, u32[]{:S(2)}, u32[]{:S(2)}) collective-permute-start(bf16[64,2048]{1,0:T(8,128)(2,1)S(1)} %constant_dynamic-slice_fusion.8.refs_0_), channel_id=1, source_target_pairs={{0,1},{1,0},{2,3},{3,2},{4,5},{5,4},{6,7},{7,6},{8,9},{9,8},{10,11... | collective-permute-start | bytes 786440 | tf_op jit(solution)/shard_map/ppermute | solution.py:486
  29.7 144.4 %all-gather.5.cloned.1.call-start = ((), (), s32[]{:S(2)}) async-start(), calls=%async_computation.1 | async-start | bytes 4456448 | tf_op jit(solution)/shard_map/all_gather | solution.py:866
  29.8 35.9 %collective-permute-start = (bf16[3,512,512]{2,1,0:T(8,128)(2,1)S(1)}, bf16[3,512,512]{2,1,0:T(8,128)(2,1)S(1)}, u32[]{:S(2)}, u32[]{:S(2)}) collective-permute-start(bf16[3,512,512]{2,1,0:T(8,128)(2,1)S(1)} %copy-done.19), channel_id=1, source_target_pairs={{0,1},{1,0},{2,3},{3,2},{4,5},{5,4},{6,7},{7,6},{8,9},{9,8},{10,11... | collective-permute-start | bytes 4718600 | tf_op jit(solution)/shard_map/ppermute | solution.py:486
  32.4 33.3 %copy-start.33 = (bf16[2,512]{1,0:T(2,128)(2,1)S(1)}, bf16[2,512]{1,0:T(2,128)(2,1)}, u32[]{:S(2)}) copy-start(bf16[2,512]{1,0:T(2,128)(2,1)} %param.22) | copy-start | bytes 6148
  32.4 33.4 %copy-start.30 = (bf16[2048]{0:T(1024)(128)(2,1)S(1)}, bf16[2048]{0:T(1024)(128)(2,1)}, u32[]{:S(2)}) copy-start(bf16[2048]{0:T(1024)(128)(2,1)} %param.28) | copy-start | bytes 12292
  65.7 3.8 collective-permute-start.1
  65.7 3.7 collective-permute-start.2
  67.2 24.6 %collective-permute-start.6 = (bf16[128,1024]{1,0:T(8,128)(2,1)S(1)}, bf16[128,1024]{1,0:T(8,128)(2,1)}, u32[]{:S(2)}, u32[]{:S(2)}) collective-permute-start(bf16[128,1024]{1,0:T(8,128)(2,1)S(1)} %constant_dynamic-slice_fusion.4), channel_id=1, source_target_pairs={{0,1},{1,0},{2,3},{3,2},{4,5},{5,4},{6,7},{7,6},{8,9},{9,8},{10,11... | collective-permute-start | bytes 786440 | tf_op jit(solution)/shard_map/ppermute | solution.py:486
  78.8 29.2 %copy-start.37 = (bf16[1024]{0:T(1024)(128)(2,1)S(1)}, bf16[1024]{0:T(1024)(128)(2,1)}, u32[]{:S(2)}) copy-start(bf16[1024]{0:T(1024)(128)(2,1)} %param.26) | copy-start | bytes 6148
  91.9 13.6 %collective-permute-start.3 = (bf16[256,1024]{1,0:T(8,128)(2,1)S(1)}, bf16[256,1024]{1,0:T(8,128)(2,1)S(1)}, u32[]{:S(2)}, u32[]{:S(2)}) collective-permute-start(bf16[256,1024]{1,0:T(8,128)(2,1)S(1)} %constant_dynamic-slice_fusion.5), channel_id=1, source_target_pairs={{0,1},{1,0},{2,3},{3,2},{4,5},{5,4},{6,7},{7,6},{8,9},{9,8},{10,11... | collective-permute-start | bytes 1572872 | tf_op jit(solution)/shard_map/ppermute | solution.py:486
  105.6 7.0 %collective-permute-start.4 = (bf16[256,1024]{1,0:T(8,128)(2,1)S(1)}, bf16[256,1024]{1,0:T(8,128)(2,1)S(1)}, u32[]{:S(2)}, u32[]{:S(2)}) collective-permute-start(bf16[256,1024]{1,0:T(8,128)(2,1)S(1)} %collective-permute-done.3), channel_id=1, source_target_pairs={{0,2},{2,0},{4,6},{6,4},{8,10},{10,8},{12,14},{14,12},{16,18},{18,... | collective-permute-start | bytes 1572872 | tf_op jit(solution)/shard_map/ppermute | solution.py:490
  155.6 6.7 %collective-permute-start.7 = (bf16[1024,1024]{1,0:T(8,128)(2,1)}, bf16[1024,1024]{1,0:T(8,128)(2,1)}, u32[]{:S(2)}, u32[]{:S(2)}) collective-permute-start(bf16[1024,1024]{1,0:T(8,128)(2,1)} %fusion.9), channel_id=1, source_target_pairs={{0,2},{2,0},{4,6},{6,4},{8,10},{10,8},{12,14},{14,12},{16,18},{18,... | collective-permute-start | bytes 6291464 | tf_op jit(solution)/shard_map/ppermute | solution.py:490
  190.9 18.3 %collective-permute-start.8 = (bf16[512,2048]{1,0:T(8,128)(2,1)}, bf16[512,2048]{1,0:T(8,128)(2,1)}, u32[]{:S(2)}, u32[]{:S(2)}) collective-permute-start(bf16[512,2048]{1,0:T(8,128)(2,1)} %convolution_convert_fusion.1), channel_id=1, source_target_pairs={{0,2},{2,0},{4,6},{6,4},{8,10},{10,8},{12,14},{14,12},{16,18},{18,... | collective-permute-start | bytes 6291464 | tf_op jit(solution)/shard_map/ppermute | solution.py:490
  194.9 146.1 %collective-permute-start.15 = (bf16[1024,1024]{1,0:T(8,128)(2,1)}, bf16[1024,1024]{1,0:T(8,128)(2,1)}, u32[]{:S(2)}, u32[]{:S(2)}) collective-permute-start(bf16[1024,1024]{1,0:T(8,128)(2,1)} %fusion.12), channel_id=1, source_target_pairs={{0,2},{2,0},{4,6},{6,4},{8,10},{10,8},{12,14},{14,12},{16,18},{18,... | collective-permute-start | bytes 6291464 | tf_op jit(solution)/shard_map/ppermute | solution.py:490
  200.4 138.6 %collective-permute-start.16 = (bf16[1024,1024]{1,0:T(8,128)(2,1)}, bf16[1024,1024]{1,0:T(8,128)(2,1)}, u32[]{:S(2)}, u32[]{:S(2)}) collective-permute-start(bf16[1024,1024]{1,0:T(8,128)(2,1)} %add_convert_fusion.3), channel_id=1, source_target_pairs={{0,1},{1,0},{2,3},{3,2},{4,5},{5,4},{6,7},{7,6},{8,9},{9,8},{10,11... | collective-permute-start | bytes 6291464 | tf_op jit(solution)/shard_map/ppermute | solution.py:486
  204.5 213.7 %collective-permute-start.17 = (bf16[512,2048]{1,0:T(8,128)(2,1)}, bf16[512,2048]{1,0:T(8,128)(2,1)}, u32[]{:S(2)}, u32[]{:S(2)}) collective-permute-start(bf16[512,2048]{1,0:T(8,128)(2,1)} %convolution_convert_fusion), channel_id=1, source_target_pairs={{0,2},{2,0},{4,6},{6,4},{8,10},{10,8},{12,14},{14,12},{16,18},{18,... | collective-permute-start | bytes 6291464 | tf_op jit(solution)/shard_map/ppermute | solution.py:490
  237.6 4.5 collective-permute-start.9
  284.1 3.6 collective-permute-start.11
  285.1 4.7 collective-permute-start.12
  287.7 5.3 collective-permute-start.13
  289.8 128.5 %collective-permute-start.18 = (bf16[512,2048]{1,0:T(8,128)(2,1)}, bf16[512,2048]{1,0:T(8,128)(2,1)}, u32[]{:S(2)}, u32[]{:S(2)}) collective-permute-start(bf16[512,2048]{1,0:T(8,128)(2,1)} %add_convert_fusion.2), channel_id=1, source_target_pairs={{0,1},{1,0},{2,3},{3,2},{4,5},{5,4},{6,7},{7,6},{8,9},{9,8},{10,11... | collective-permute-start | bytes 6291464 | tf_op jit(solution)/shard_map/ppermute | solution.py:486
  293.0 59.3 %collective-permute-start.19 = (bf16[256,1024]{1,0:T(8,128)(2,1)}, bf16[256,1024]{1,0:T(8,128)(2,1)}, u32[]{:S(2)}, u32[]{:S(2)}) collective-permute-start(bf16[256,1024]{1,0:T(8,128)(2,1)} %convolution_convert_fusion.5), channel_id=1, source_target_pairs={{0,2},{2,0},{4,6},{6,4},{8,10},{10,8},{12,14},{14,12},{16,18},{18,... | collective-permute-start | bytes 1572872 | tf_op jit(solution)/shard_map/ppermute | solution.py:490
  339.0 15.1 %collective-permute-start.20 = (bf16[256,1024]{1,0:T(8,128)(2,1)}, bf16[256,1024]{1,0:T(8,128)(2,1)S(1)}, u32[]{:S(2)}, u32[]{:S(2)}) collective-permute-start(bf16[256,1024]{1,0:T(8,128)(2,1)} %add_convert_fusion.13.tie_ref), channel_id=1, source_target_pairs={{0,1},{1,0},{2,3},{3,2},{4,5},{5,4},{6,7},{7,6},{8,9},{9,8},{10,11... | collective-permute-start | bytes 1572872 | tf_op jit(solution)/shard_map/ppermute | solution.py:486
  341.0 35.5 %collective-permute-start.10 = (bf16[512,1024]{1,0:T(8,128)(2,1)S(1)}, bf16[512,1024]{1,0:T(8,128)(2,1)S(1)}, u32[]{:S(2)}, u32[]{:S(2)}) collective-permute-start(bf16[512,1024]{1,0:T(8,128)(2,1)S(1)} %copy-done.23), channel_id=1, source_target_pairs={{0,1},{1,0},{2,3},{3,2},{4,5},{5,4},{6,7},{7,6},{8,9},{9,8},{10,11... | collective-permute-start | bytes 3145736 | tf_op jit(solution)/shard_map/ppermute | solution.py:486
  352.4 35.5 %collective-permute-start.22 = (bf16[512,512]{1,0:T(8,128)(2,1)S(1)}, bf16[512,512]{1,0:T(8,128)(2,1)}, u32[]{:S(2)}, u32[]{:S(2)}) collective-permute-start(bf16[512,512]{1,0:T(8,128)(2,1)S(1)} %copy-done.40), channel_id=1, source_target_pairs={{0,1},{1,0},{2,3},{3,2},{4,5},{5,4},{6,7},{7,6},{8,9},{9,8},{10,11... | collective-permute-start | bytes 1572872 | tf_op jit(solution)/shard_map/ppermute | solution.py:486
  354.0 45.0 %collective-permute-start.24 = (bf16[512,512]{1,0:T(8,128)(2,1)}, bf16[512,512]{1,0:T(8,128)(2,1)}, u32[]{:S(2)}, u32[]{:S(2)}) collective-permute-start(bf16[512,512]{1,0:T(8,128)(2,1)} %add_convert_fusion.11), channel_id=1, source_target_pairs={{0,1},{1,0},{2,3},{3,2},{4,5},{5,4},{6,7},{7,6},{8,9},{9,8},{10,11... | collective-permute-start | bytes 1572872 | tf_op jit(solution)/shard_map/ppermute | solution.py:486
  376.5 33.3 %collective-permute-start.26 = (bf16[512,512]{1,0:T(8,128)(2,1)}, bf16[512,512]{1,0:T(8,128)(2,1)}, u32[]{:S(2)}, u32[]{:S(2)}) collective-permute-start(bf16[512,512]{1,0:T(8,128)(2,1)} %add_convert_fusion.10), channel_id=1, source_target_pairs={{0,1},{1,0},{2,3},{3,2},{4,5},{5,4},{6,7},{7,6},{8,9},{9,8},{10,11... | collective-permute-start | bytes 1572872 | tf_op jit(solution)/shard_map/ppermute | solution.py:486
  387.9 23.4 %collective-permute-start.21 = (bf16[512,512]{1,0:T(8,128)(2,1)}, bf16[512,512]{1,0:T(8,128)(2,1)}, u32[]{:S(2)}, u32[]{:S(2)}) collective-permute-start(bf16[512,512]{1,0:T(8,128)(2,1)} %convolution_convert_fusion.9.refs_0_), channel_id=1, source_target_pairs={{0,2},{2,0},{4,6},{6,4},{8,10},{10,8},{12,14},{14,12},{16,18},{18,... | collective-permute-start | bytes 1572872 | tf_op jit(solution)/shard_map/ppermute | solution.py:490
  399.1 14.9 %collective-permute-start.23 = (bf16[512,512]{1,0:T(8,128)(2,1)}, bf16[512,512]{1,0:T(8,128)(2,1)S(1)}, u32[]{:S(2)}, u32[]{:S(2)}) collective-permute-start(bf16[512,512]{1,0:T(8,128)(2,1)} %convolution_convert_fusion.8.refs_1_), channel_id=1, source_target_pairs={{0,2},{2,0},{4,6},{6,4},{8,10},{10,8},{12,14},{14,12},{16,18},{18,... | collective-permute-start | bytes 1572872 | tf_op jit(solution)/shard_map/ppermute | solution.py:490
  409.8 6.4 %collective-permute-start.25 = (bf16[512,512]{1,0:T(8,128)(2,1)S(1)}, bf16[512,512]{1,0:T(8,128)(2,1)S(1)}, u32[]{:S(2)}, u32[]{:S(2)}) collective-permute-start(bf16[512,512]{1,0:T(8,128)(2,1)S(1)} %copy-done.39), channel_id=1, source_target_pairs={{0,2},{2,0},{4,6},{6,4},{8,10},{10,8},{12,14},{14,12},{16,18},{18,... | collective-permute-start | bytes 1572872 | tf_op jit(solution)/shard_map/ppermute | solution.py:490
  411.3 172.7 %collective-permute-start.14 = (bf16[512,1024]{1,0:T(8,128)(2,1)}, bf16[512,1024]{1,0:T(8,128)(2,1)S(1)}, u32[]{:S(2)}, u32[]{:S(2)}) collective-permute-start(bf16[512,1024]{1,0:T(8,128)(2,1)} %constant_dynamic-slice_fusion.2), channel_id=1, source_target_pairs={{0,1},{1,0},{2,3},{3,2},{4,5},{5,4},{6,7},{7,6},{8,9},{9,8},{10,11... | collective-permute-start | bytes 3145736 | tf_op jit(solution)/shard_map/ppermute | solution.py:486
  (54 other events, 360.0 us)
Sparse Core Ops, SparseCore 0:
  29.8 50.7 all-gather.2
  92.0 50.6 all-gather.4
where the time goes:
time: 603 us; the launch traced here: 593 us
  Pallas kernels  299 us (50%)
  matrix products  94.9 us (16%)
  waiting for transfers between devices  84.4 us (14%)
  other arithmetic  68.2 us (11%)
  local copies, waits for them, and re-layouts  17.8 us (3%)
  between operations  15 us (2%)
  starting transfers between devices  13.9 us (2%)
    pallas_call x1, Pallas kernels, plane_sums(): pl.pallas_call(functools.partial(ring_kernel, blocks, cuts, small is not...  139 us
    ppermute x13, waiting for transfers between devices, to_tensor(): return lax.ppermute(value, 'tensor', [(0, 1), (1, 0)])  84.3 us
    dot_general x24, matrix products, contract_rows(): lax.dot_general(left, right, (((0,), (0,)), ((), ())), preferred_element_...  70.3 us
    pallas_call x5, Pallas kernels, over_rows(): pl.pallas_call(kernel, grid_spec=pltpu.PrefetchScalarGridSpec(num_scalar_...  67.5 us
    pallas_call x2, Pallas kernels, attention_grads(): pl.pallas_call(backward_kernel, grid=(pairs,), out_shape=(shape, shape, s...  40 us
    pallas_call x2, Pallas kernels, activations(): pl.pallas_call(act_kernel, grid=(hidden // columns,), in_specs=[whole_spe...  26.9 us
    pallas_call x2, Pallas kernels, attention_out(): pl.pallas_call(forward_kernel, grid=(pairs,), out_shape=(jax.ShapeDtypeSt...  25.9 us
    convert_element_type x6, other arithmetic, pair_grad(): (part + more.astype(jnp.float32)).astype(jnp.bfloat16)  19.5 us
  transfers between devices with their start and end apart: 29, of which 8 were waited for; matrix products, arithmetic and copies ran while one was open for 27% of the time, Pallas kernels for 50%

commit v1 on v0

--- a/solution.py
+++ b/solution.py
@@ -338,7 +338,8 @@
     )(query, keys, values, mixed, grad, levels, lanes, rows)
 
 
-ROW_BLOCK = 256
+ROW_BLOCK = 512
+PART = 256
 
 
 def whole_spec(array):
@@ -374,35 +375,50 @@
     )(facts, *arrays)
 
 
+def parts():
+    return [pl.ds(start, PART) for start in range(0, ROW_BLOCK, PART)]
+
+
 def project_kernel(facts, tok_ref, gain_ref, shift_ref, w_ref, bias_ref, *refs):
     norm_ref, q_ref, k_ref, v_ref = refs[-4:]
-    normal, _ = norm_parts(tok_ref[0].astype(jnp.float32))
-    normed = (normal * gain_ref[...] + shift_ref[...]).astype(jnp.bfloat16)
-    norm_ref[...] = normed
-    q_ref[...] = (mm(normed, w_ref[0]) + bias_ref[0:1, :]).astype(jnp.bfloat16)
-    k_ref[...] = mm(normed, w_ref[1]).astype(jnp.bfloat16)
-    v_ref[...] = (mm(normed, w_ref[2]) + bias_ref[1:2, :]).astype(jnp.bfloat16)
+    for at in parts():
+        normal, _ = norm_parts(tok_ref[0, at, :].astype(jnp.float32))
+        normed = (normal * gain_ref[...] + shift_ref[...]).astype(jnp.bfloat16)
+        norm_ref[at, :] = normed
+        q_ref[at, :] = (mm(normed, w_ref[0]) + bias_ref[0:1, :]).astype(jnp.bfloat16)
+        k_ref[at, :] = mm(normed, w_ref[1]).astype(jnp.bfloat16)
+        v_ref[at, :] = (mm(normed, w_ref[2]) + bias_ref[1:2, :]).astype(jnp.bfloat16)
 
 
 def hidden_kernel(
     facts, tok_ref, a0_ref, a1_ref, w0_ref, w1_ref, bias_ref, gain_ref, shift_ref, hid_ref, norm_ref
 ):
-    hidden = tok_ref[0].astype(jnp.float32) + bias_ref[...]
-    hidden = hidden + mm(a0_ref[...], w0_ref[...]) + mm(a1_ref[...], w1_ref[...])
-    hid_ref[...] = hidden
-    normal, _ = norm_parts(hidden)
-    norm_ref[...] = (normal * gain_ref[...] + shift_ref[...]).astype(jnp.bfloat16)
+    for at in parts():
+        hidden = tok_ref[0, at, :].astype(jnp.float32) + bias_ref[...]
+        hidden = hidden + mm(a0_ref[at, :], w0_ref[...]) + mm(a1_ref[at, :], w1_ref[...])
+        hid_ref[at, :] = hidden
+        normal, _ = norm_parts(hidden)
+        norm_ref[at, :] = (normal * gain_ref[...] + shift_ref[...]).astype(jnp.bfloat16)
+
+
+def act_parts(pre):
+    square = pre * pre
+    first = root_two_pi * pre * (1.0 + 0.044715 * square)
+    half = 0.5 + 0.5 * jnp.tanh(first)
+    value = pre * half
+    steep = (2.0 * root_two_pi) + (6.0 * 0.044715 * root_two_pi) * square
+    return value, half + value * (1.0 - half) * steep
 
 
 def act_kernel(norm_ref, w_ref, bias_ref, act_ref, slope_ref):
     def rows(number, carry):
-        at = pl.ds(pl.multiple_of(number * ROW_BLOCK, ROW_BLOCK), ROW_BLOCK)
-        value, slope = gelu_parts(mm(norm_ref[at, :], w_ref[...]) + bias_ref[...])
+        at = pl.ds(pl.multiple_of(number * PART, PART), PART)
+        value, slope = act_parts(mm(norm_ref[at, :], w_ref[...]) + bias_ref[...])
         act_ref[at, :] = value.astype(jnp.bfloat16)
         slope_ref[at, :] = slope.astype(jnp.bfloat16)
         return carry
 
-    lax.fori_loop(0, norm_ref.shape[0] // ROW_BLOCK, rows, 0, unroll=True)
+    lax.fori_loop(0, norm_ref.shape[0] // PART, rows, 0, unroll=True)
 
 
 def activations(normed, weight, bias):
@@ -431,15 +447,19 @@
 
 
 def output_kernel(facts, hid_ref, a0_ref, a1_ref, w0_ref, w1_ref, bias_ref, tie_ref, out_ref):
-    total = hid_ref[...] + bias_ref[...] + mm(a0_ref[...], w0_ref[...])
-    out_ref[...] = (total + mm(a1_ref[...], w1_ref[...])).astype(jnp.bfloat16)
-
-
-def add_sums(sums_ref, rows):
+    for at in parts():
+        total = hid_ref[at, :] + bias_ref[...] + mm(a0_ref[at, :], w0_ref[...])
+        out_ref[at, :] = (total + mm(a1_ref[at, :], w1_ref[...])).astype(jnp.bfloat16)
+
+
+def clear_sums(*refs):
     @pl.when(pl.program_id(0) == 0)
     def _():
-        sums_ref[...] = jnp.zeros_like(sums_ref)
-
+        for ref in refs:
+            ref[...] = jnp.zeros_like(ref)
+
+
+def add_sums(sums_ref, rows):
     for index, value in enumerate(rows):
         sums_ref[index : index + 1, :] += jnp.sum(value, 0, keepdims=True)
 
@@ -447,15 +467,18 @@
 def hidden_grad_kernel(
     facts, g0_ref, g1_ref, w0_ref, w1_ref, hid_ref, gain_ref, dout_ref, grad_ref, one_ref, sums_ref
 ):
-    grad_norm = mm(g0_ref[...], w0_ref[...], NT) + mm(g1_ref[...], w1_ref[...], NT)
-    normal, inverse = norm_parts(hid_ref[...])
-    place = lax.broadcasted_iota(jnp.int32, grad_norm.shape, 0) + pl.program_id(0) * ROW_BLOCK
-    grad_out = jnp.where(place < facts[1], dout_ref[0].astype(jnp.float32), 0.0)
-    grad = grad_out + norm_backward(grad_norm, normal, inverse, gain_ref[...])
-    one = grad.astype(jnp.bfloat16)
-    grad_ref[...] = grad
-    one_ref[...] = one
-    add_sums(sums_ref, [grad_norm * normal, grad_norm, one.astype(jnp.float32), grad_out])
+    clear_sums(sums_ref)
+    for at in parts():
+        grad_norm = mm(g0_ref[at, :], w0_ref[...], NT) + mm(g1_ref[at, :], w1_ref[...], NT)
+        normal, inverse = norm_parts(hid_ref[at, :])
+        first = pl.program_id(0) * ROW_BLOCK + at.start
+        place = lax.broadcasted_iota(jnp.int32, grad_norm.shape, 0) + first
+        grad_out = jnp.where(place < facts[1], dout_ref[0, at, :].astype(jnp.float32), 0.0)
+        grad = grad_out + norm_backward(grad_norm, normal, inverse, gain_ref[...])
+        one = grad.astype(jnp.bfloat16)
+        grad_ref[at, :] = grad
+        one_ref[at, :] = one
+        add_sums(sums_ref, [grad_norm * normal, grad_norm, one.astype(jnp.float32), grad_out])
 
 
 def token_grad_kernel(
@@ -463,16 +486,20 @@
     gain_ref, *refs,
 ):
     out_ref, sums_ref, heads_ref = refs[-3:]
-    grad_norm = None
-    for refs, weight in (((q0_ref, k0_ref, v0_ref), w0_ref), ((q1_ref, k1_ref, v1_ref), w1_ref)):
-        for part, ref in enumerate(refs):
-            more = mm(ref[...], weight[part], NT)
-            grad_norm = more if grad_norm is None else grad_norm + more
-    normal, inverse = norm_parts(tok_ref[0].astype(jnp.float32))
-    grad = grad_ref[...] + norm_backward(grad_norm, normal, inverse, gain_ref[...])
-    out_ref[...] = grad.astype(jnp.bfloat16)
-    add_sums(sums_ref, [grad_norm * normal, grad_norm])
-    add_sums(heads_ref, [ref[...].astype(jnp.float32) for ref in (q0_ref, q1_ref, v0_ref, v1_ref)])
+    clear_sums(sums_ref, heads_ref)
+    halves = (((q0_ref, k0_ref, v0_ref), w0_ref), ((q1_ref, k1_ref, v1_ref), w1_ref))
+    for at in parts():
+        grad_norm = None
+        for sources, weight in halves:
+            for part, ref in enumerate(sources):
+                more = mm(ref[at, :], weight[part], NT)
+                grad_norm = more if grad_norm is None else grad_norm + more
+        normal, inverse = norm_parts(tok_ref[0, at, :].astype(jnp.float32))
+        grad = grad_ref[at, :] + norm_backward(grad_norm, normal, inverse, gain_ref[...])
+        out_ref[at, :] = grad.astype(jnp.bfloat16)
+        add_sums(sums_ref, [grad_norm * normal, grad_norm])
+        heads = [ref[at, :].astype(jnp.float32) for ref in (q0_ref, q1_ref, v0_ref, v1_ref)]
+        add_sums(heads_ref, heads)
 
 
 RING = ((0, 0), (1, 0), (2, 0), (3, 0), (3, 1), (2, 1), (1, 1), (0, 1))
@@ -641,19 +668,25 @@
     return scratch + [pltpu.SemaphoreType.DMA((streams, count))] * 2
 
 
-def ring_kernel(blocks, cuts, has_small, has_tie, *refs):
+def ring_kernel(blocks, cuts, has_small, has_tie, has_swap, *refs):
     values, refs = refs[:blocks], refs[blocks:]
     if has_small:
         small_ref, refs = refs[0], refs[1:]
     refs = refs[has_tie:]
+    if has_swap:
+        lone_ref, refs = refs[0], refs[1:]
     results, refs = refs[:blocks], refs[blocks:]
     if has_small:
         small_out, refs = refs[0], refs[1:]
+    if has_swap:
+        lone_out, refs = refs[0], refs[1:]
     slots, refs = refs[:blocks], refs[blocks:]
     sums, refs = refs[:blocks], refs[blocks:]
     ring = Ring(values, slots, sums, results, refs[:4], cuts)
+    refs = refs[4:]
     if has_small:
-        small_slots, small_sums, small_send_sems, small_recv_sems = refs[4:]
+        small_slots, small_sums, small_send_sems, small_recv_sems = refs[:4]
+        refs = refs[4:]
         device, y, z = ring.device, ring.y, ring.z
         small_targets = [
             ring.partner,
@@ -688,18 +721,32 @@
     ring.first()
     if has_small:
         exchange(0).start()
+    if has_swap:
+        lone_send_sem, lone_recv_sem = refs
+        lone = pltpu.make_async_remote_copy(
+            src_ref=lone_ref,
+            dst_ref=lone_out.at[ring.core],
+            send_sem=lone_send_sem,
+            recv_sem=lone_recv_sem,
+            device_id=ring.partner,
+            device_id_type=pl.DeviceIdType.MESH,
+        )
+        lone.start()
+        lone_out[ring.core] = lone_ref[...]
     for step in range(1, 2 * ring.count - 2):
         if has_small and step % 2 == 0 and step // 2 <= len(small_targets):
             take_exchange(step // 2 - 1)
         ring.hop(step)
     ring.last()
     ring.drain()
+    if has_swap:
+        lone.wait()
     if has_small:
         for turn in range(len(small_targets)):
             exchange(turn).wait_send()
 
 
-def plane_sums(values, identity, small=None, tie=None, cuts=1):
+def plane_sums(values, identity, small=None, tie=None, lone=None, cuts=1):
     blocks = len(values)
     shaped = [ring_shape(value) for value in values]
     size = sum(value.size for value in values)
@@ -716,8 +763,14 @@
     if tie is not None:
         inputs.append(tie)
         in_specs.append(pl.BlockSpec(memory_space=pl.ANY))
+    if lone is not None:
+        inputs.append(lone)
+        in_specs.append(vmem)
+        shapes.append(jax.ShapeDtypeStruct((2, *lone.shape), lone.dtype))
+        scratch += [pltpu.SemaphoreType.DMA] * 2
+    flags = (small is not None, int(tie is not None), lone is not None)
     results = pl.pallas_call(
-        functools.partial(ring_kernel, blocks, cuts, small is not None, int(tie is not None)),
+        functools.partial(ring_kernel, blocks, cuts, *flags),
         out_shape=shapes,
         in_specs=in_specs,
         out_specs=[vmem] * len(shapes),
@@ -729,7 +782,7 @@
     sums = [
         result.reshape(2 * value.shape[0], value.shape[1]) for result, value in zip(results, values)
     ]
-    return sums if small is None else (sums, results[-1])
+    return [*sums, *results[blocks:]]
 
 
 def core_send(left, rights, core):
@@ -895,6 +948,11 @@
     left_up, right_up = (normed_two, normed_two), ([grad_pre[0]], [grad_pre[1]])
     local_up, passed_up, sent = start_grad(left_up, right_up, core)
     late_pre = lax.optimization_barrier((*grad_pre, *sent))
+    (mine_down,) = pair_grad(
+        left_down[0], right_down[0], local_down, passed_down, core, *sent
+    )
+    planes = [list(range(core_at, 2 * len(RING), 2)) for core_at in range(2)]
+    sum_down = lax.psum(mine_down, "dp", axis_index_groups=planes)
     grad_hidden, grad_one, sums_two = run(
         hidden_grad_kernel,
         [by_row(late_pre[0]), by_row(late_pre[1]), fixed(up[0]), fixed(up[1]), by_row(hidden)]
@@ -950,12 +1008,12 @@
     )
     small = jnp.pad(small, ((0, 16 - small.shape[0]), (0, 0)))
     mine = [
-        *pair_grad(left_down[0], right_down[0], local_down, passed_down, core, done),
         *pair_grad(left_up[0], right_up[0], local_up, passed_up, core, done),
         *pair_grad(left_out[0], right_out[0], local_out, passed_out, core, done),
         *pair_grad(normed_one, grads[0], local_qkv, passed_qkv, core, done),
     ]
-    (grad_wdown, grad_wup, grad_wout, *grad_wqkv), small = plane_sums(mine, 1, small)
+    grad_wup, grad_wout, *grad_wqkv, small, grad_wdown = plane_sums(mine, 1, small, lone=sum_down)
+    grad_wdown = grad_wdown.reshape(2 * grad_wdown.shape[1], width)
     grad_wqkv = jnp.stack(grad_wqkv, 0).astype(f32)
     wide = [lax.dynamic_slice_in_dim(small[i], own * local_width, local_width, 0) for i in (6, 7)]
     grad_bup = lax.dynamic_slice_in_dim(

time: 603 us -> 561 us (0.930)
  Pallas kernels: 299 us -> 259 us
  waiting for transfers between devices: 84.4 us -> 66.9 us
  matrix products: 94.9 us -> 110 us
    pallas_call x1, Pallas kernels: 139 us -> 99 us  [plane_sums(): pl.pallas_call(functools.partial(ring_kernel, blocks, cuts, *flags), out_...]
    ppermute x13, waiting for transfers between devices: 84.3 us -> 66.9 us  [to_tensor(): return lax.ppermute(value, 'tensor', [(0, 1), (1, 0)])]
    dot_general x4, matrix products: 17.8 us -> 28.9 us  [contract_cols(): lax.dot_general(left, right, (((1,), (1,)), ((), ())), preferred_element_...]
  transfers between devices with their start and end apart: 29 -> 30, of which waited for: 8 -> 7; matrix products, arithmetic and copies ran while one was open for 27% -> 31% of each run, Pallas kernels for 50% -> 47%
where the time goes in v1:
time: 561 us; the launch traced here: 551 us
  Pallas kernels  259 us (46%)
  matrix products  110 us (20%)
  other arithmetic  67 us (12%)
  waiting for transfers between devices  66.9 us (12%)
  local copies, waits for them, and re-layouts  17.5 us (3%)
  starting transfers between devices  15.3 us (3%)
  between operations  14.6 us (3%)
    pallas_call x1, Pallas kernels, plane_sums(): pl.pallas_call(functools.partial(ring_kernel, blocks, cuts, *flags), out_...  99 us
    dot_general x24, matrix products, contract_rows(): lax.dot_general(left, right, (((0,), (0,)), ((), ())), preferred_element_...  74.9 us
    pallas_call x5, Pallas kernels, over_rows(): pl.pallas_call(kernel, grid_spec=pltpu.PrefetchScalarGridSpec(num_scalar_...  70 us
    ppermute x13, waiting for transfers between devices, to_tensor(): return lax.ppermute(value, 'tensor', [(0, 1), (1, 0)])  66.9 us
    pallas_call x2, Pallas kernels, attention_grads(): pl.pallas_call(backward_kernel, grid=(pairs,), out_shape=(shape, shape, s...  39.8 us
    dot_general x4, matrix products, contract_cols(): lax.dot_general(left, right, (((1,), (1,)), ((), ())), preferred_element_...  28.9 us
    pallas_call x2, Pallas kernels, attention_out(): pl.pallas_call(forward_kernel, grid=(pairs,), out_shape=(jax.ShapeDtypeSt...  25.9 us
    pallas_call x2, Pallas kernels, activations(): pl.pallas_call(act_kernel, grid=(hidden // columns,), in_specs=[whole_spe...  24.5 us
  transfers between devices with their start and end apart: 30, of which 7 were waited for; matrix products, arithmetic and copies ran while one was open for 31% of the time, Pallas kernels for 47%

profile of v1, /device:TPU:0, one launch (start us, length us, event | category | flops | bytes accessed | tf_op | source)
XLA Modules:
  0.0 551.0 jit_solution(18132639151252302935)
XLA Ops:
  20.2 8.3 %shard_map.263 = (bf16[1024,1024]{1,0:T(8,128)(2,1)}, bf16[1024,512]{1,0:T(8,128)(2,1)}, bf16[1024,512]{1,0:T(8,128)(2,1)}, bf16[1024,512]{1,0:T(8,128)(2,1)}) custom-call(s32[2]{0:T(128)} %pad_add_fusion.facts, bf16[2,1024,1024]{2,1,0:T(8,128)(2,1)} %tok_ref.5, f32[1,1024]{1,0:T(1,128)} %bitcast.140, f32[1,1024]{1,0:T(1,128)} %bitcast.143, ...), custom_call_target="tpu_custom_call" | custom-call | flops 3221225472 | bytes 9187328 | tf_op jit(solution)/shard_map/pallas_call | solution.py:361
  31.9 12.9 %attention_out.2 = (bf16[1024,512]{1,0:T(8,128)(2,1)}, f32[4,8,1024]{2,1,0:T(8,128)}) custom-call(bf16[1024,512]{1,0:T(8,128)(2,1)} %get-tuple-element.67.q_ref, bf16[1024,512]{1,0:T(8,128)(2,1)} %get-tuple-element.68.k_ref, bf16[1024,512]{1,0:T(8,128)(2,1)} %get-tuple-element.69.v_ref, bf16[1024,128]{1,0:T(8,128)(2,1)} %select_convert_fusion.lanes_ref, ...), custom_call_target="tpu_custom_call" | custom-call | flops 4294967296 | bytes 4194304 | tf_op jit(solution)/shard_map/attention_out/pallas_call | solution.py:300
  44.8 20.4 %collective-permute-done = bf16[3,512,512]{2,1,0:T(8,128)(2,1)S(1)} collective-permute-done((bf16[3,512,512]{2,1,0:T(8,128)(2,1)S(1)}, bf16[3,512,512]{2,1,0:T(8,128)(2,1)S(1)}, u32[]{:S(2)}, u32[]{:S(2)}) %collective-permute-start) | collective-permute-done | bytes 1572896 | tf_op jit(solution)/shard_map/ppermute | solution.py:513
  78.4 13.0 %attention_out.3 = (bf16[1024,512]{1,0:T(8,128)(2,1)}, f32[4,8,1024]{2,1,0:T(8,128)}) custom-call(bf16[1024,512]{1,0:T(8,128)(2,1)} %add_convert_fusion.5.q_ref, bf16[1024,512]{1,0:T(8,128)(2,1)} %convolution_convert_fusion.4.k_ref, bf16[1024,512]{1,0:T(8,128)(2,1)} %add_convert_fusion.4.v_ref, bf16[1024,128]{1,0:T(8,128)(2,1)} %select_convert_fusion.lanes_ref, ...), custom_call_target="tpu_custom_call" | custom-call | flops 4294967296 | bytes 4194304 | tf_op jit(solution)/shard_map/attention_out/pallas_call | solution.py:300
  91.8 13.3 %collective-permute-done.3 = bf16[256,1024]{1,0:T(8,128)(2,1)S(1)} collective-permute-done((bf16[256,1024]{1,0:T(8,128)(2,1)S(1)}, bf16[256,1024]{1,0:T(8,128)(2,1)S(1)}, u32[]{:S(2)}, u32[]{:S(2)}) %collective-permute-start.3) | collective-permute-done | bytes 524320 | tf_op jit(solution)/shard_map/ppermute | solution.py:513
  114.1 8.0 %shard_map.264 = (f32[1024,1024]{1,0:T(8,128)}, bf16[1024,1024]{1,0:T(8,128)(2,1)}) custom-call(s32[2]{0:T(128)} %pad_add_fusion.facts, bf16[2,1024,1024]{2,1,0:T(8,128)(2,1)} %tok_ref.5, bf16[1024,512]{1,0:T(8,128)(2,1)} %get-tuple-element.70.a0_ref.o_ref, bf16[1024,512]{1,0:T(8,128)(2,1)} %get-tuple-element.73.a1_ref.o_ref, bf16[512,1024]{1,0:T(8,128)(2,1)} %w0_ref.3, ...), custom_call_target="tpu_custom_call" | custom-call | flops 2147483648 | bytes 8400896 | tf_op jit(solution)/shard_map/pallas_call | solution.py:361
  122.0 12.2 %activations.2 = (bf16[1024,2048]{1,0:T(8,128)(2,1)}, bf16[1024,2048]{1,0:T(8,128)(2,1)}) custom-call(bf16[1024,1024]{1,0:T(8,128)(2,1)} %get-tuple-element.77.norm_ref, bf16[1024,2048]{1,0:T(8,128)(2,1)} %w0_ref.4, f32[1,2048]{1,0:T(1,128)} %bitcast.127), custom_call_target="tpu_custom_call" | custom-call | flops 4294967296 | bytes 16777216 | tf_op jit(solution)/shard_map/activations/pallas_call | solution.py:430
  134.2 12.3 %activations.3 = (bf16[1024,2048]{1,0:T(8,128)(2,1)}, bf16[1024,2048]{1,0:T(8,128)(2,1)}) custom-call(bf16[1024,1024]{1,0:T(8,128)(2,1)} %get-tuple-element.77.norm_ref, bf16[1024,2048]{1,0:T(8,128)(2,1)} %all-gather.3.cloned.1.call-done.w_ref.w1_ref, f32[1,2048]{1,0:T(1,128)} %bitcast.128), custom_call_target="tpu_custom_call" | custom-call | flops 4294967296 | bytes 16777216 | tf_op jit(solution)/shard_map/activations/pallas_call | solution.py:430
  146.5 5.9 %fusion.9 = bf16[1024,1024]{1,0:T(8,128)(2,1)} fusion(bf16[1024,1024]{1,0:T(8,128)(2,1)} %fusion, bf16[1024,2048]{1,0:T(8,128)(2,1)} %get-tuple-element.81.a1_ref, s32[]{:T(128)S(6)} %select_n.250), kind=kOutput, calls=%fused_computation.34 | convolution fusion | flops 2148532224 | bytes 6291460 | tf_op jit(solution)/shard_map/dot_general | solution.py:26
  153.0 6.1 %fusion.12 = bf16[1024,1024]{1,0:T(8,128)(2,1)} fusion(bf16[1024,1024]{1,0:T(8,128)(2,1)} %fusion, bf16[1024,2048]{1,0:T(8,128)(2,1)} %get-tuple-element.78.a0_ref, s32[]{:T(128)S(6)} %select_n.250), kind=kOutput, calls=%fused_computation.35 | convolution fusion | flops 2148532224 | bytes 6291460 | tf_op jit(solution)/shard_map/dot_general | solution.py:26
  159.1 5.5 %add_convert_fusion.3 = bf16[1024,1024]{1,0:T(8,128)(2,1)} fusion(bf16[1024,1024]{1,0:T(8,128)(2,1)} %collective-permute-done.7, bf16[1024,1024]{1,0:T(8,128)(2,1)S(1)} %copy-done.13, bf16[1024,2048]{1,0:T(8,128)(2,1)S(1)} %copy-done.54, s32[]{:T(128)S(6)} %select_n.249), kind=kOutput, calls=%fused_computation.19 | convolution fusion | flops 2150629376 | bytes 8388612 | tf_op jit(solution)/shard_map/dot_general | solution.py:26
  164.7 17.3 %convert_reduce_fusion.1 = (f32[2048]{0:T(1024)S(1)}, bf16[1024,2048]{1,0:T(8,128)(2,1)}) fusion(bf16[1024,2048]{1,0:T(8,128)(2,1)S(1)} %copy-done.55, bf16[1024,1024]{1,0:T(8,128)(2,1)S(1)} %copy-done.13, bf16[2048,1024]{1,0:T(8,128)(2,1)S(1)} %copy-done.31), kind=kOutput, calls=%fused_computation.1 | convolution fusion | flops 4305451008 | bytes 14688256 | tf_op jit(solution)/shard_map/dot_general | solution.py:32
  182.0 7.0 %fusion.112 = f32[1024,2048]{1,0:T(8,128)S(1)} fusion(bf16[1024,1024]{1,0:T(8,128)(2,1)} %fusion, bf16[2048,1024]{1,0:T(8,128)(2,1)} %all-gather.5.cloned.1.call-done.w1_ref), kind=kOutput, calls=%fused_computation.178 | convolution fusion | flops 4294967296 | bytes 14680064 | tf_op jit(solution)/shard_map/dot_general | solution.py:32
  192.9 5.8 %convolution_convert_fusion.1 = bf16[512,2048]{1,0:T(8,128)(2,1)} fusion(bf16[1024,2048]{1,0:T(8,128)(2,1)S(1)} %get-tuple-element.89.g1_ref, bf16[1024,1024]{1,0:T(8,128)(2,1)} %get-tuple-element.77.norm_ref, s32[]{:T(128)S(6)} %select_n.251), kind=kOutput, calls=%fused_computation.21 | convolution fusion | flops 2148532224 | bytes 7340036 | tf_op jit(solution)/shard_map/dot_general | solution.py:26
  203.7 4.5 fusion.1
  208.5 3.9 convolution_convert_fusion
  212.5 4.5 fusion.34
  217.0 6.9 %add_convert_fusion.2 = bf16[512,2048]{1,0:T(8,128)(2,1)} fusion(bf16[512,2048]{1,0:T(8,128)(2,1)} %collective-permute-done.8, bf16[1024,2048]{1,0:T(8,128)(2,1)} %copy-done.1, bf16[1024,1024]{1,0:T(8,128)(2,1)S(1)} %copy-done.27, s32[]{:T(128)S(6)} %select_n.231), kind=kOutput, calls=%fused_computation.18 | convolution fusion | flops 2150629376 | bytes 9437188 | tf_op jit(solution)/shard_map/dot_general | solution.py:26
  225.6 20.5 %shard_map.265 = (f32[1024,1024]{1,0:T(8,128)}, bf16[1024,1024]{1,0:T(8,128)(2,1)}, f32[8,1024]{1,0:T(8,128)}) custom-call(s32[2]{0:T(128)} %pad_add_fusion.facts, bf16[1024,2048]{1,0:T(8,128)(2,1)} %get-tuple-element.88.g0_ref, bf16[1024,2048]{1,0:T(8,128)(2,1)} %copy-done.1, bf16[1024,2048]{1,0:T(8,128)(2,1)} %w0_ref.4, ...), custom_call_target="tpu_custom_call" | custom-call | flops 8589934592 | bytes 25169920 | tf_op jit(solution)/shard_map/pallas_call | solution.py:361
  251.2 5.8 %collective-permute-done.26 = bf16[1024,1024]{1,0:T(8,128)(2,1)} collective-permute-done((bf16[1024,1024]{1,0:T(8,128)(2,1)}, bf16[1024,1024]{1,0:T(8,128)(2,1)}, u32[]{:S(2)}, u32[]{:S(2)}) %collective-permute-start.26) | collective-permute-done | bytes 2097184 | tf_op jit(solution)/shard_map/ppermute | solution.py:513
  257.0 4.8 add_convert_fusion
  266.3 17.3 %shard_map.266 = bf16[1024,1024]{1,0:T(8,128)(2,1)} custom-call(s32[2]{0:T(128)} %pad_add_fusion.facts, f32[1024,1024]{1,0:T(8,128)} %get-tuple-element.76.hid_ref, bf16[1024,2048]{1,0:T(8,128)(2,1)} %get-tuple-element.78.a0_ref, bf16[1024,2048]{1,0:T(8,128)(2,1)} %get-tuple-element.81.a1_ref, bf16[2048,1024]{1,0:T(8,128)(2,1)} %w0_ref.5, ...), custom_call_target="tpu_custom_call" | custom-call | flops 8589934592 | bytes 21499904 | tf_op jit(solution)/shard_map/pallas_call | solution.py:361
  285.8 19.9 %attention_grads.2 = (bf16[1024,512]{1,0:T(8,128)(2,1)}, bf16[1024,512]{1,0:T(8,128)(2,1)}, bf16[1024,512]{1,0:T(8,128)(2,1)}) custom-call(bf16[1024,512]{1,0:T(8,128)(2,1)} %add_convert_fusion.5.q_ref, bf16[1024,512]{1,0:T(8,128)(2,1)} %convolution_convert_fusion.4.k_ref, bf16[1024,512]{1,0:T(8,128)(2,1)} %add_convert_fusion.4.v_ref, ...), custom_call_target="tpu_custom_call" | custom-call | flops 10737418240 | bytes 7340032 | tf_op jit(solution)/shard_map/attention_grads/pallas_call | solution.py:324
  321.6 19.8 %attention_grads.3 = (bf16[1024,512]{1,0:T(8,128)(2,1)}, bf16[1024,512]{1,0:T(8,128)(2,1)}, bf16[1024,512]{1,0:T(8,128)(2,1)}) custom-call(bf16[1024,512]{1,0:T(8,128)(2,1)} %get-tuple-element.67.q_ref, bf16[1024,512]{1,0:T(8,128)(2,1)} %get-tuple-element.68.k_ref, bf16[1024,512]{1,0:T(8,128)(2,1)} %get-tuple-element.69.v_ref, ...), custom_call_target="tpu_custom_call" | custom-call | flops 10737418240 | bytes 7340032 | tf_op jit(solution)/shard_map/attention_grads/pallas_call | solution.py:324
  349.2 16.0 %shard_map.267 = (bf16[1024,1024]{1,0:T(8,128)(2,1)}, f32[8,1024]{1,0:T(8,128)}, f32[8,512]{1,0:T(8,128)}) custom-call(s32[2]{0:T(128)} %pad_add_fusion.facts, bf16[1024,512]{1,0:T(8,128)(2,1)} %get-tuple-element.98.q0_ref, bf16[1024,512]{1,0:T(8,128)(2,1)} %get-tuple-element.99.k0_ref, bf16[1024,512]{1,0:T(8,128)(2,1)} %get-tuple-element.100.v0_ref, ...), custom_call_target="tpu_custom_call" | custom-call | flops 6442450944 | bytes 22548480 | tf_op jit(solution)/shard_map/pallas_call | solution.py:361
  377.6 8.8 %collective-permute-done.20 = bf16[512,512]{1,0:T(8,128)(2,1)} collective-permute-done((bf16[512,512]{1,0:T(8,128)(2,1)S(1)}, bf16[512,512]{1,0:T(8,128)(2,1)}, u32[]{:S(2)}, u32[]{:S(2)}) %collective-permute-start.20) | collective-permute-done | bytes 524320 | tf_op jit(solution)/shard_map/ppermute | solution.py:513
  387.9 9.8 %collective-permute-done.22 = bf16[512,512]{1,0:T(8,128)(2,1)} collective-permute-done((bf16[512,512]{1,0:T(8,128)(2,1)}, bf16[512,512]{1,0:T(8,128)(2,1)}, u32[]{:S(2)}, u32[]{:S(2)}) %collective-permute-start.22) | collective-permute-done | bytes 524320 | tf_op jit(solution)/shard_map/ppermute | solution.py:513
  399.4 8.1 %collective-permute-done.24 = bf16[512,512]{1,0:T(8,128)(2,1)} collective-permute-done((bf16[512,512]{1,0:T(8,128)(2,1)}, bf16[512,512]{1,0:T(8,128)(2,1)}, u32[]{:S(2)}, u32[]{:S(2)}) %collective-permute-start.24) | collective-permute-done | bytes 524320 | tf_op jit(solution)/shard_map/ppermute | solution.py:513
  416.3 4.7 add_convert_fusion.1
  421.0 99.0 %plane_sums.1 = (bf16[2,2,8,32,2048]{4,3,2,1,0:T(8,128)(2,1)}, bf16[2,2,8,16,1024]{4,3,2,1,0:T(8,128)(2,1)}, bf16[2,2,8,32,512]{4,3,2,1,0:T(8,128)(2,1)}, bf16[2...) custom-call(bf16[2,8,32,2048]{3,2,1,0:T(8,128)(2,1)} %bitcast.109, ...), custom_call_target="tpu_custom_call" | custom-call | flops 2097152 | bytes 12582912 | tf_op jit(solution)/shard_map/plane_sums/pallas_call | solution.py:772
  525.3 6.8 %bitcast_convert_fusion.1 = f32[1024,2048]{1,0:T(8,128)} fusion(bf16[2,2,8,32,2048]{4,3,2,1,0:T(8,128)(2,1)} %get-tuple-element.118), kind=kLoop, calls=%fused_computation.13 | loop fusion | flops 2097152 | bytes 12582912 | tf_op jit(solution)/shard_map/convert_element_type | solution.py:1033
  537.3 4.7 bitcast_convert_fusion
  (251 shorter events, 122.4 us)
Async XLA Ops:
  7.2 127.1 %all-gather.3.cloned.1.call-start = ((), (), s32[]{:S(2)}) async-start(), calls=%async_computation | async-start | bytes 4456448 | tf_op jit(solution)/shard_map/all_gather | solution.py:909
  8.2 20.3 %collective-permute-start.5 = (bf16[64,2048]{1,0:T(8,128)(2,1)S(1)}, bf16[64,2048]{1,0:T(8,128)(2,1)S(1)}, u32[]{:S(2)}, u32[]{:S(2)}) collective-permute-start(bf16[64,2048]{1,0:T(8,128)(2,1)S(1)} %constant_dynamic-slice_fusion.8.refs_0_), channel_id=1, source_target_pairs={{0,1},{1,0},{2,3},{3,2},{4,5},{5,4},{6,7},{7,6},{8,9},{9,8},{10,11... | collective-permute-start | bytes 786440 | tf_op jit(solution)/shard_map/ppermute | solution.py:513
  29.3 152.7 %all-gather.5.cloned.1.call-start = ((), (), s32[]{:S(2)}) async-start(), calls=%async_computation.1 | async-start | bytes 4456448 | tf_op jit(solution)/shard_map/all_gather | solution.py:919
  29.3 35.9 %collective-permute-start = (bf16[3,512,512]{2,1,0:T(8,128)(2,1)S(1)}, bf16[3,512,512]{2,1,0:T(8,128)(2,1)S(1)}, u32[]{:S(2)}, u32[]{:S(2)}) collective-permute-start(bf16[3,512,512]{2,1,0:T(8,128)(2,1)S(1)} %copy-done.20), channel_id=1, source_target_pairs={{0,1},{1,0},{2,3},{3,2},{4,5},{5,4},{6,7},{7,6},{8,9},{9,8},{10,11... | collective-permute-start | bytes 4718600 | tf_op jit(solution)/shard_map/ppermute | solution.py:513
  31.9 33.3 %copy-start.33 = (bf16[2,512]{1,0:T(2,128)(2,1)S(1)}, bf16[2,512]{1,0:T(2,128)(2,1)}, u32[]{:S(2)}) copy-start(bf16[2,512]{1,0:T(2,128)(2,1)} %param.22) | copy-start | bytes 6148
  31.9 33.4 %copy-start.30 = (bf16[2048]{0:T(1024)(128)(2,1)S(1)}, bf16[2048]{0:T(1024)(128)(2,1)}, u32[]{:S(2)}) copy-start(bf16[2048]{0:T(1024)(128)(2,1)} %param.28) | copy-start | bytes 12292
  65.3 3.8 collective-permute-start.1
  65.3 3.7 collective-permute-start.2
  66.8 24.6 %collective-permute-start.6 = (bf16[128,1024]{1,0:T(8,128)(2,1)S(1)}, bf16[128,1024]{1,0:T(8,128)(2,1)}, u32[]{:S(2)}, u32[]{:S(2)}) collective-permute-start(bf16[128,1024]{1,0:T(8,128)(2,1)S(1)} %constant_dynamic-slice_fusion.4), channel_id=1, source_target_pairs={{0,1},{1,0},{2,3},{3,2},{4,5},{5,4},{6,7},{7,6},{8,9},{9,8},{10,11... | collective-permute-start | bytes 786440 | tf_op jit(solution)/shard_map/ppermute | solution.py:513
  91.4 329.6 %all-reduce.3.cloned.1.call-start = ((), (), s32[]{:S(2)}) async-start(), calls=%async_computation.2 | async-start | bytes 4194304 | tf_op jit(solution)/shard_map/psum | solution.py:955
  91.5 13.6 %collective-permute-start.3 = (bf16[256,1024]{1,0:T(8,128)(2,1)S(1)}, bf16[256,1024]{1,0:T(8,128)(2,1)S(1)}, u32[]{:S(2)}, u32[]{:S(2)}) collective-permute-start(bf16[256,1024]{1,0:T(8,128)(2,1)S(1)} %constant_dynamic-slice_fusion.5), channel_id=1, source_target_pairs={{0,1},{1,0},{2,3},{3,2},{4,5},{5,4},{6,7},{7,6},{8,9},{9,8},{10,11... | collective-permute-start | bytes 1572872 | tf_op jit(solution)/shard_map/ppermute | solution.py:513
  105.2 7.0 %collective-permute-start.4 = (bf16[256,1024]{1,0:T(8,128)(2,1)S(1)}, bf16[256,1024]{1,0:T(8,128)(2,1)S(1)}, u32[]{:S(2)}, u32[]{:S(2)}) collective-permute-start(bf16[256,1024]{1,0:T(8,128)(2,1)S(1)} %collective-permute-done.3), channel_id=1, source_target_pairs={{0,2},{2,0},{4,6},{6,4},{8,10},{10,8},{12,14},{14,12},{16,18},{18,... | collective-permute-start | bytes 1572872 | tf_op jit(solution)/shard_map/ppermute | solution.py:517
  152.5 6.6 %collective-permute-start.7 = (bf16[1024,1024]{1,0:T(8,128)(2,1)}, bf16[1024,1024]{1,0:T(8,128)(2,1)}, u32[]{:S(2)}, u32[]{:S(2)}) collective-permute-start(bf16[1024,1024]{1,0:T(8,128)(2,1)} %fusion.9), channel_id=1, source_target_pairs={{0,2},{2,0},{4,6},{6,4},{8,10},{10,8},{12,14},{14,12},{16,18},{18,... | collective-permute-start | bytes 6291464 | tf_op jit(solution)/shard_map/ppermute | solution.py:517
  198.7 18.3 %collective-permute-start.8 = (bf16[512,2048]{1,0:T(8,128)(2,1)}, bf16[512,2048]{1,0:T(8,128)(2,1)}, u32[]{:S(2)}, u32[]{:S(2)}) collective-permute-start(bf16[512,2048]{1,0:T(8,128)(2,1)} %convolution_convert_fusion.1), channel_id=1, source_target_pairs={{0,2},{2,0},{4,6},{6,4},{8,10},{10,8},{12,14},{14,12},{16,18},{18,... | collective-permute-start | bytes 6291464 | tf_op jit(solution)/shard_map/ppermute | solution.py:517
  202.7 54.3 %collective-permute-start.25 = (bf16[1024,1024]{1,0:T(8,128)(2,1)}, bf16[1024,1024]{1,0:T(8,128)(2,1)}, u32[]{:S(2)}, u32[]{:S(2)}) collective-permute-start(bf16[1024,1024]{1,0:T(8,128)(2,1)} %fusion.12), channel_id=1, source_target_pairs={{0,2},{2,0},{4,6},{6,4},{8,10},{10,8},{12,14},{14,12},{16,18},{18,... | collective-permute-start | bytes 6291464 | tf_op jit(solution)/shard_map/ppermute | solution.py:517
  208.2 48.8 %collective-permute-start.26 = (bf16[1024,1024]{1,0:T(8,128)(2,1)}, bf16[1024,1024]{1,0:T(8,128)(2,1)}, u32[]{:S(2)}, u32[]{:S(2)}) collective-permute-start(bf16[1024,1024]{1,0:T(8,128)(2,1)} %add_convert_fusion.3), channel_id=1, source_target_pairs={{0,1},{1,0},{2,3},{3,2},{4,5},{5,4},{6,7},{7,6},{8,9},{9,8},{10,11... | collective-permute-start | bytes 6291464 | tf_op jit(solution)/shard_map/ppermute | solution.py:513
  212.3 203.9 %collective-permute-start.15 = (bf16[512,2048]{1,0:T(8,128)(2,1)}, bf16[512,2048]{1,0:T(8,128)(2,1)}, u32[]{:S(2)}, u32[]{:S(2)}) collective-permute-start(bf16[512,2048]{1,0:T(8,128)(2,1)} %convolution_convert_fusion), channel_id=1, source_target_pairs={{0,2},{2,0},{4,6},{6,4},{8,10},{10,8},{12,14},{14,12},{16,18},{18,... | collective-permute-start | bytes 6291464 | tf_op jit(solution)/shard_map/ppermute | solution.py:517
  223.9 192.4 %collective-permute-start.16 = (bf16[512,2048]{1,0:T(8,128)(2,1)}, bf16[512,2048]{1,0:T(8,128)(2,1)}, u32[]{:S(2)}, u32[]{:S(2)}) collective-permute-start(bf16[512,2048]{1,0:T(8,128)(2,1)} %add_convert_fusion.2), channel_id=1, source_target_pairs={{0,1},{1,0},{2,3},{3,2},{4,5},{5,4},{6,7},{7,6},{8,9},{9,8},{10,11... | collective-permute-start | bytes 6291464 | tf_op jit(solution)/shard_map/ppermute | solution.py:513
  249.5 14.1 %collective-permute-start.9 = (bf16[256,1024]{1,0:T(8,128)(2,1)}, bf16[256,1024]{1,0:T(8,128)(2,1)}, u32[]{:S(2)}, u32[]{:S(2)}) collective-permute-start(bf16[256,1024]{1,0:T(8,128)(2,1)} %convolution_convert_fusion.6), channel_id=1, source_target_pairs={{0,2},{2,0},{4,6},{6,4},{8,10},{10,8},{12,14},{14,12},{16,18},{18,... | collective-permute-start | bytes 1572872 | tf_op jit(solution)/shard_map/ppermute | solution.py:517
  257.0 114.4 %collective-permute-start.17 = (bf16[256,1024]{1,0:T(8,128)(2,1)}, bf16[256,1024]{1,0:T(8,128)(2,1)}, u32[]{:S(2)}, u32[]{:S(2)}) collective-permute-start(bf16[256,1024]{1,0:T(8,128)(2,1)} %convolution_convert_fusion.5), channel_id=1, source_target_pairs={{0,2},{2,0},{4,6},{6,4},{8,10},{10,8},{12,14},{14,12},{16,18},{18,... | collective-permute-start | bytes 1572872 | tf_op jit(solution)/shard_map/ppermute | solution.py:517
  308.2 3.9 collective-permute-start.11
  309.5 4.7 collective-permute-start.12
  312.2 4.3 collective-permute-start.13
  314.2 58.1 %collective-permute-start.18 = (bf16[256,1024]{1,0:T(8,128)(2,1)}, bf16[256,1024]{1,0:T(8,128)(2,1)}, u32[]{:S(2)}, u32[]{:S(2)}) collective-permute-start(bf16[256,1024]{1,0:T(8,128)(2,1)} %add_convert_fusion.13.tie_ref), channel_id=1, source_target_pairs={{0,1},{1,0},{2,3},{3,2},{4,5},{5,4},{6,7},{7,6},{8,9},{9,8},{10,11... | collective-permute-start | bytes 1572872 | tf_op jit(solution)/shard_map/ppermute | solution.py:513
  316.4 60.4 %collective-permute-start.10 = (bf16[512,1024]{1,0:T(8,128)(2,1)}, bf16[512,1024]{1,0:T(8,128)(2,1)S(1)}, u32[]{:S(2)}, u32[]{:S(2)}) collective-permute-start(bf16[512,1024]{1,0:T(8,128)(2,1)} %constant_dynamic-slice_fusion.3), channel_id=1, source_target_pairs={{0,1},{1,0},{2,3},{3,2},{4,5},{5,4},{6,7},{7,6},{8,9},{9,8},{10,11... | collective-permute-start | bytes 3145736 | tf_op jit(solution)/shard_map/ppermute | solution.py:513
  371.5 15.0 %collective-permute-start.20 = (bf16[512,512]{1,0:T(8,128)(2,1)S(1)}, bf16[512,512]{1,0:T(8,128)(2,1)}, u32[]{:S(2)}, u32[]{:S(2)}) collective-permute-start(bf16[512,512]{1,0:T(8,128)(2,1)S(1)} %copy-done.41), channel_id=1, source_target_pairs={{0,1},{1,0},{2,3},{3,2},{4,5},{5,4},{6,7},{7,6},{8,9},{9,8},{10,11... | collective-permute-start | bytes 1572872 | tf_op jit(solution)/shard_map/ppermute | solution.py:513
  372.3 25.4 %collective-permute-start.22 = (bf16[512,512]{1,0:T(8,128)(2,1)}, bf16[512,512]{1,0:T(8,128)(2,1)}, u32[]{:S(2)}, u32[]{:S(2)}) collective-permute-start(bf16[512,512]{1,0:T(8,128)(2,1)} %add_convert_fusion.11), channel_id=1, source_target_pairs={{0,1},{1,0},{2,3},{3,2},{4,5},{5,4},{6,7},{7,6},{8,9},{9,8},{10,11... | collective-permute-start | bytes 1572872 | tf_op jit(solution)/shard_map/ppermute | solution.py:513
  376.8 30.7 %collective-permute-start.24 = (bf16[512,512]{1,0:T(8,128)(2,1)}, bf16[512,512]{1,0:T(8,128)(2,1)}, u32[]{:S(2)}, u32[]{:S(2)}) collective-permute-start(bf16[512,512]{1,0:T(8,128)(2,1)} %add_convert_fusion.10), channel_id=1, source_target_pairs={{0,1},{1,0},{2,3},{3,2},{4,5},{5,4},{6,7},{7,6},{8,9},{9,8},{10,11... | collective-permute-start | bytes 1572872 | tf_op jit(solution)/shard_map/ppermute | solution.py:513
  386.4 22.6 %collective-permute-start.19 = (bf16[512,512]{1,0:T(8,128)(2,1)}, bf16[512,512]{1,0:T(8,128)(2,1)}, u32[]{:S(2)}, u32[]{:S(2)}) collective-permute-start(bf16[512,512]{1,0:T(8,128)(2,1)} %convolution_convert_fusion.9.refs_0_), channel_id=1, source_target_pairs={{0,2},{2,0},{4,6},{6,4},{8,10},{10,8},{12,14},{14,12},{16,18},{18,... | collective-permute-start | bytes 1572872 | tf_op jit(solution)/shard_map/ppermute | solution.py:517
  397.7 14.4 %collective-permute-start.21 = (bf16[512,512]{1,0:T(8,128)(2,1)}, bf16[512,512]{1,0:T(8,128)(2,1)S(1)}, u32[]{:S(2)}, u32[]{:S(2)}) collective-permute-start(bf16[512,512]{1,0:T(8,128)(2,1)} %convolution_convert_fusion.8.refs_1_), channel_id=1, source_target_pairs={{0,2},{2,0},{4,6},{6,4},{8,10},{10,8},{12,14},{14,12},{16,18},{18,... | collective-permute-start | bytes 1572872 | tf_op jit(solution)/shard_map/ppermute | solution.py:517
  407.5 6.7 %collective-permute-start.23 = (bf16[512,512]{1,0:T(8,128)(2,1)S(1)}, bf16[512,512]{1,0:T(8,128)(2,1)S(1)}, u32[]{:S(2)}, u32[]{:S(2)}) collective-permute-start(bf16[512,512]{1,0:T(8,128)(2,1)S(1)} %copy-done.40), channel_id=1, source_target_pairs={{0,2},{2,0},{4,6},{6,4},{8,10},{10,8},{12,14},{14,12},{16,18},{18,... | collective-permute-start | bytes 1572872 | tf_op jit(solution)/shard_map/ppermute | solution.py:517
  409.1 133.0 %collective-permute-start.14 = (bf16[512,1024]{1,0:T(8,128)(2,1)}, bf16[512,1024]{1,0:T(8,128)(2,1)S(1)}, u32[]{:S(2)}, u32[]{:S(2)}) collective-permute-start(bf16[512,1024]{1,0:T(8,128)(2,1)} %constant_dynamic-slice_fusion.2), channel_id=1, source_target_pairs={{0,1},{1,0},{2,3},{3,2},{4,5},{5,4},{6,7},{7,6},{8,9},{9,8},{10,11... | collective-permute-start | bytes 3145736 | tf_op jit(solution)/shard_map/ppermute | solution.py:513
  (54 other events, 411.5 us)
Sparse Core Ops, SparseCore 0:
  29.4 50.6 all-gather.2
  91.5 50.6 all-gather.4
  262.0 102.8 all-reduce.2
